TPU v7x, 32 devices: a whole 2x2x4 slice. The times are simulated.
32 devices in a mesh: grid: 8 (over y, x, core), ao: 4 (over z).
Axes of the slice: x: 2, y: 2, z: 4, core: 2. Of those that a mesh axis runs over, the one named last changes fastest.
Arguments:
- trial: bfloat16 [12288, 16, 2, 128], P('ao'), may hold values from -0.15625 to 0.15625
- occupied: bfloat16 [12288, 2, 128], P('ao'), may hold values from -0.15625 to 0.15625
- colloc: bfloat16 [32, 128, 1536], P('grid'), may hold values from -3 to 3
- blocks: int32 [32, 12], P('grid'), may hold values from 0 to 95, as said below
- coords: float32 [32, 3, 128], P('grid'), may hold values from 0 to 4
- weights: float32 [32, 128], P('grid'), may hold values from 0.02 to 0.2
Outputs:
- exchange: float32 [16, 12288, 2, 128], P('ao', 'grid')
Inputs may be any that keep to these rules, and one draw needn't show every extreme that they name: The 12 blocks of a batch are distinct and lie among 24 cyclically consecutive shell blocks.
All inputs are finite; a program needn't handle non-finite values.
Results may differ from a plain program's by a relative error of at most 0.0053.
Values may be sent and summed in bfloat16 or wider, within the bound.
No kernel may reach another device: no remote copies, remote signals or barrier semaphores. Data moves between devices by JAX's collectives and lax.ppermute only.
A program may use at most 192 MiB of HBM per device.

v0:
```python
import functools

import jax
import jax.numpy as jnp
from jax import lax
from jax.experimental import pallas as pl
from jax.experimental.pallas import tpu as pltpu
from jax.sharding import PartitionSpec as P

F32 = jnp.float32
BF16 = jnp.bfloat16
EXTRA = 16
PARAMS = pltpu.CompilerParams(vmem_limit_bytes=58 * 1024 * 1024)
SMEM = pl.BlockSpec(memory_space=pltpu.SMEM)
VMEM = pl.BlockSpec(memory_space=pltpu.VMEM)
ANY = pl.BlockSpec(memory_space=pl.ANY)


def kernel_matrix(points, quad):
    differ = points[..., :, None, :] - points[..., :, :, None]
    square = jnp.sum(differ * differ, axis=-3)
    return quad[..., :, None] * quad[..., None, :] / jnp.sqrt(square + 0.25)


def selectors(blk):
    ao = lax.broadcasted_iota(jnp.int32, (blk, 2 * blk), 0)
    col = lax.broadcasted_iota(jnp.int32, (blk, 2 * blk), 1)
    return [(col == 2 * ao + c).astype(F32).astype(BF16) for c in range(2)]


def pack_kernel(where, trial, *refs):
    outs, (rows, sem) = refs[:-2], refs[-2:]
    nb, blk, width = outs[0].shape
    nocc = width // 2
    copies = []
    for i in range(len(outs)):
        for j in range(nb):
            at = (where[0] + j) * blk
            copies.append(
                pltpu.make_async_copy(trial.at[pl.ds(at, blk), where[1 + i]], rows.at[i, j], sem.at[i, j])
            )
    for c in copies:
        c.start()
    pick = selectors(blk)
    for i, out in enumerate(outs):
        for j in range(nb):
            copies[i * nb + j].wait()
            both = rows[i, j].reshape(2 * blk, nocc)
            for c in range(2):
                split = jnp.dot(pick[c], both, preferred_element_type=F32)
                out[j, :, c * nocc : (c + 1) * nocc] = split.astype(BF16)


def pack(trial, where, planes, nb, blk):
    nocc = trial.shape[3]
    return pl.pallas_call(
        pack_kernel,
        out_shape=(jax.ShapeDtypeStruct((nb, blk, 2 * nocc), BF16),) * planes,
        in_specs=[SMEM, ANY],
        out_specs=(VMEM,) * planes,
        scratch_shapes=[pltpu.VMEM((planes, nb, blk, 2, nocc), BF16), pltpu.SemaphoreType.DMA((planes, nb))],
        compiler_params=PARAMS,
        name="pack",
    )(where, trial)


def occupied_kernel(ids, meta, occupied, values, keep, send, table):
    batches, sig = ids.shape
    blk, nocc = occupied.shape[0] // (table.shape[0] - 1), occupied.shape[2]
    nlocal = table.shape[0] - 1
    pick = selectors(blk)
    for j in range(nlocal):
        both = occupied[j * blk : (j + 1) * blk].reshape(2 * blk, nocc)
        for c in range(2):
            split = jnp.dot(pick[c], both, preferred_element_type=F32)
            table[j, :, c * nocc : (c + 1) * nocc] = split.astype(BF16)
    table[nlocal] = jnp.zeros(table.shape[1:], BF16)

    def block(b, s):
        local = ids[b, s] - meta[0]
        return table[jnp.where((local >= 0) & (local < nlocal), local, nlocal)]

    for b in range(batches):
        total = jnp.zeros(keep.shape[1:], F32)
        for s in range(0, sig, 2):
            two = jnp.concatenate([block(b, s), block(b, s + 1)], axis=0)
            total += jnp.dot(values[b, :, s * blk : (s + 2) * blk], two, preferred_element_type=F32)
        keep[b] = total
        send[b] = total.astype(BF16)


def occupied_part(occupied, colloc, blocks, meta, blk):
    batches, npts, _ = colloc.shape
    nocc = occupied.shape[2]
    shape = (batches, npts, 2 * nocc)
    return pl.pallas_call(
        occupied_kernel,
        out_shape=(jax.ShapeDtypeStruct(shape, F32), jax.ShapeDtypeStruct(shape, BF16)),
        in_specs=[SMEM, SMEM, VMEM, VMEM],
        out_specs=(VMEM, VMEM),
        scratch_shapes=[pltpu.VMEM((occupied.shape[0] // blk + 1, blk, 2 * nocc), BF16)],
        compiler_params=PARAMS,
        name="occupied",
    )(blocks, meta, occupied, colloc)


def potential_kernel(sizes, ids, meta, *refs):
    nt, tmasks, npiece, xmasks, no, omasks, first, count, nlocal, rank = sizes
    panels, refs = refs[:nt], refs[nt:]
    values, refs = refs[:npiece], refs[npiece:]
    occ, refs = refs[:no], refs[no:]
    kern, out, table, x, sems = refs
    nb, blk, width = panels[0].shape
    nocc = width // 2
    npts = x.shape[2]
    sig = ids.shape[2]
    copies = []
    for i in range(nt):
        over, side = tmasks[i]
        at = (meta[3] ^ over) * nlocal + (meta[4] ^ side) * nb
        copies.append(pltpu.make_async_copy(panels[i], table.at[pl.ds(at, nb)], sems.at[i]))
    place = 0
    for i in range(npiece):
        size = values[i].shape[0]
        copies.append(
            pltpu.make_async_copy(values[i].at[:, :, pl.ds(0, npts)], x.at[pl.ds(place, size)], sems.at[nt + i])
        )
        place += size
    for c in copies:
        c.start()
    for c in copies:
        c.wait()
    sources = [m for masks in xmasks for m in masks]
    where = {m: (i, j) for i, masks in enumerate(omasks) for j, m in enumerate(masks)}
    dims = (((1,), (1,)), ((), ()))
    for p, mask in enumerate(sources):
        piece, row = where[mask]
        for b in range(count):
            dens = jnp.zeros((npts, width), F32)
            for s in range(0, sig, 2):
                panel = jnp.concatenate([table[ids[p, b, s]], table[ids[p, b, s + 1]]], axis=0)
                dens += jnp.dot(x[p, b, :, s * blk : (s + 2) * blk], panel, preferred_element_type=F32)
            left = dens.astype(BF16)
            og = occ[piece][row, first + b]
            oreal, oimag = og[:, :nocc], og[:, nocc:]
            turn = jnp.concatenate([og, jnp.concatenate([-oimag, oreal], axis=1)], axis=0)
            rho = lax.dot_general(left, turn, dims, preferred_element_type=F32)
            weight = kern[p, b]
            m = (rho * jnp.concatenate([weight, weight], axis=1)).astype(BF16)
            out[meta[5] ^ (mask // rank), b] = jnp.dot(m, turn, preferred_element_type=F32).astype(BF16)


def potential(panels, values, occ, kern, ids, meta, first, nlocal, rank):
    tmasks = tuple(m for _, m in panels)
    xmasks = tuple(tuple(m) for _, m in values)
    omasks = tuple(tuple(m) for _, m in occ)
    nsrc, count, sig = ids.shape
    npts = kern.shape[-1]
    blk, width = panels[0][0].shape[1:]
    nt, npiece, no = len(panels), len(values), len(occ)
    total = nlocal * (nt * panels[0][0].shape[0] // nlocal)
    sizes = (nt, tmasks, npiece, xmasks, no, omasks, first, count, nlocal, rank)
    return pl.pallas_call(
        functools.partial(potential_kernel, sizes),
        out_shape=jax.ShapeDtypeStruct((nsrc, count, npts, width), BF16),
        in_specs=[SMEM, SMEM] + [ANY] * (nt + npiece) + [VMEM] * (no + 1),
        out_specs=VMEM,
        scratch_shapes=[
            pltpu.VMEM((total, blk, width), BF16),
            pltpu.VMEM((nsrc, count, npts, sig * blk), BF16),
            pltpu.SemaphoreType.DMA((nt + npiece,)),
        ],
        compiler_params=PARAMS,
        name="potential",
    )(ids, meta, *[a for a, _ in panels], *[a for a, _ in values], *[a for a, _ in occ], kern)


def select_kernel(sizes, *refs):
    ncall, xmasks, rank, nown = sizes
    all_ids, refs = refs[:ncall], refs[ncall:]
    meta, refs = refs[0], refs[1:]
    flat = [m for masks in xmasks for m in masks]
    values, (facts, columns, x, sems) = refs[: len(flat)], refs[len(flat) :]
    ncount = all_ids[0].shape[1]
    sig = all_ids[0].shape[2]
    npts = x.shape[2]
    blk = x.shape[3] // sig
    copies = []
    place = 0
    starts = []
    for i, piece in enumerate(values):
        size = piece.shape[0]
        copies.append(pltpu.make_async_copy(piece.at[:, :, pl.ds(0, npts)], x.at[pl.ds(place, size)], sems.at[i]))
        starts.append(place)
        place += size
    for c in copies:
        c.start()
    for c in copies:
        c.wait()
    n = jnp.int32(0)
    place = 0
    groups = len(values) // ncall
    for chunk in range(ncall):
        p = 0
        for i in range(groups):
            piece = chunk * groups + i
            for j, mask in enumerate(flat[piece]):
                for b in range(ncount):

                    def one(s, n, chunk=chunk, p=p, mask=mask, b=b, row=starts[piece] + j):
                        own = all_ids[chunk][p, b, s] - meta[2]
                        mine = (own >= 0) & (own < nown)

                        @pl.when(mine)
                        def _():
                            facts[0, n] = own
                            facts[1, n] = chunk
                            facts[2, n] = mask % rank
                            facts[3, n] = meta[5] ^ (mask // rank)
                            facts[4, n] = b
                            at = pl.multiple_of(s * blk, blk)
                            columns[n] = x[row, b, :, pl.ds(at, blk)].T

                        return n + mine.astype(jnp.int32)

                    n = lax.fori_loop(0, sig, one, n)
                p += 1
    facts[5, 0] = n


def select(values, all_ids, meta, rank, nown, npts):
    flat = [piece for pieces in values for piece in pieces]
    xmasks = tuple((tuple(m),) for _, m in flat)
    nsrc, count, sig = all_ids[0].shape
    blk = flat[0][0].shape[-1] // sig
    most = len(values) * nsrc * count * sig
    sizes = (len(values), tuple(tuple(m) for m in xmasks), rank, nown)
    return pl.pallas_call(
        functools.partial(select_kernel, sizes),
        out_shape=(jax.ShapeDtypeStruct((6, most), jnp.int32), jax.ShapeDtypeStruct((most, blk, npts), BF16)),
        in_specs=[SMEM] * (len(values) + 1) + [ANY] * len(flat),
        out_specs=(SMEM, VMEM),
        scratch_shapes=[
            pltpu.VMEM((len(values) * nsrc, count, npts, sig * blk), BF16),
            pltpu.SemaphoreType.DMA((len(flat),)),
        ],
        compiler_params=PARAMS,
        name="select",
    )(*all_ids, meta, *[a for a, _ in flat])


def project_kernel(sizes, facts, meta, columns, *refs):
    nchunk, emasks, rank, group, last = sizes
    ne = len(emasks)
    potentials, refs = refs[:ne], refs[ne:]
    before = refs[0] if last else None
    out, x, e, acc, esems, xsems = refs[last:]
    nvs = e.shape[2]
    blk = x.shape[1]
    nown = acc.shape[1]
    n = facts[5, 0]
    ncopy = columns.shape[0] // group
    ecopies = []
    place = {}
    for i in range(ne):
        chunk, masks = emasks[i]
        for j, mask in enumerate(masks):
            k = place.setdefault((chunk, mask % rank), [])
            ecopies.append(
                pltpu.make_async_copy(
                    potentials[i].at[j], e.at[chunk, mask % rank, len(k)], esems.at[len(ecopies)]
                )
            )
            k.append(mask // rank)
    if last:
        ecopies.append(pltpu.make_async_copy(before, acc, esems.at[len(ecopies)]))
    xcopies = [
        pltpu.make_async_copy(columns.at[pl.ds(i * group, group)], x.at[pl.ds(i * group, group)], xsems.at[i])
        for i in range(ncopy)
    ]
    for i, c in enumerate(xcopies):

        @pl.when(i * group < n)
        def _(c=c):
            c.start()

    for c in ecopies:
        c.start()
    if not last:
        acc[...] = jnp.zeros_like(acc)
    for i, c in enumerate(xcopies):

        @pl.when(i * group < n)
        def _(c=c):
            c.wait()

    for c in ecopies:
        c.wait()

    def one(i, carry):
        own, chunk, side, source, b = [facts[f, i] for f in range(5)]
        for k in range(nvs):
            off = jnp.int32(place[(0, 0)][k])
            for other in range(1, nchunk):
                off = jnp.where(chunk == other, place[(other, 0)][k], off)
            vec = meta[5] ^ off
            acc[vec, own] += jnp.dot(x[i], e[chunk, side, k, source, b], preferred_element_type=F32)
        return carry

    lax.fori_loop(0, n, one, 0)
    if last:
        nocc = out.shape[2]
        for v in range(out.shape[0]):
            for o in range(nown):
                for c in range(2):
                    out[v, pl.ds(o * 2 * blk + c, blk, stride=2), :] = acc[v, o, :, c * nocc : (c + 1) * nocc]
    else:
        out[...] = acc[...]


def project(potentials, facts, columns, meta, before, rank, nown, group):
    emasks = tuple((chunk, tuple(m)) for chunk, _, m in potentials)
    nchunk = 1 + max(chunk for chunk, _, _ in potentials)
    nv, count, npts, width = potentials[0][1].shape[1:]
    blk = columns.shape[1]
    ne = len(potentials)
    slots = sum(len(m) for _, m in emasks) // nchunk // rank
    last = before is not None
    shape = (nv, nown * blk * 2, width // 2) if last else (nv, nown, blk, width)
    args = [facts, meta, columns, *[a for _, a, _ in potentials]] + ([before] if last else [])
    return pl.pallas_call(
        functools.partial(project_kernel, (nchunk, emasks, rank, group, int(last))),
        out_shape=jax.ShapeDtypeStruct(shape, F32),
        in_specs=[SMEM] * 2 + [ANY] * (1 + ne + int(last)),
        out_specs=VMEM,
        scratch_shapes=[
            pltpu.VMEM(columns.shape, BF16),
            pltpu.VMEM((nchunk, rank, slots, nv, count, npts, width), BF16),
            pltpu.VMEM((nv, nown, blk, width), F32),
            pltpu.SemaphoreType.DMA((sum(len(m) for _, m in emasks) + 1,)),
            pltpu.SemaphoreType.DMA((columns.shape[0] // group,)),
        ],
        compiler_params=PARAMS,
        name="project",
    )(*args)


def swap(array, axis, bit):
    size = lax.axis_size(axis)
    return lax.ppermute(array, axis, [(i, i ^ bit) for i in range(size)])


def across(pieces, bits):
    for i, bit in enumerate(bits):
        got = [(swap(a, "grid", bit), [m ^ bit for m in masks]) for a, masks in pieces]
        if i + 1 < len(bits):
            pieces = [
                (jnp.concatenate([a, b], axis=0), masks + more) for (a, masks), (b, more) in zip(pieces, got, strict=True)
            ]
        else:
            pieces = pieces + got
    return pieces


def within(pieces, bits):
    for bit in bits:
        pieces = pieces + [(swap(a, "grid", bit), [m ^ bit for m in masks]) for a, masks in pieces]
    return pieces


def thirds(x):
    high = lax.reduce_precision(x, 8, 7)
    rest = x - high
    mid = lax.reduce_precision(rest, 8, 7)
    return [high, mid, rest - mid]


def on_device(trial, occupied, colloc, blocks, coords, weights):
    n_ao, n_grid = lax.axis_size("ao"), lax.axis_size("grid")
    batches, npts, span = colloc.shape
    sig = blocks.shape[1]
    blk = span // sig
    nvec, nocc = trial.shape[1], trial.shape[3]
    nv = nvec // n_ao
    rank = n_grid // nv
    nlocal = trial.shape[0] // blk
    nown = nlocal * n_ao // n_grid
    parts = min(rank, nlocal & -nlocal)
    nb = nlocal // parts
    count = batches // 2
    ao, grid = lax.axis_index("ao"), lax.axis_index("grid")
    vector, side = grid // rank, grid % parts
    meta = jnp.stack([ao * nlocal, ao * 0, grid * nown, ao, side, vector]).astype(jnp.int32)
    high_bits = [rank << b for b in range(nv.bit_length() - 1)]
    low_bits = [1 << b for b in range(rank.bit_length() - 1)]
    part_bits = [1 << b for b in range(parts.bit_length() - 1)]

    planes = list(reversed(range(n_ao)))
    where = jnp.stack([side * nb] + [(ao ^ over) * nv + vector for over in planes]).astype(jnp.int32)
    rows = pack(trial, where, n_ao, nb, blk)
    panels = []
    for over, one in zip(planes, rows, strict=True):
        panels.append((swap(one, "ao", over) if over else one, (over, 0)))
    own = panels[-1][0]

    own, colloc, blocks = lax.optimization_barrier((own, colloc, blocks))
    panels[-1] = (own, panels[-1][1])
    numbers = [blocks % 128, blocks // 128]
    numbers = [jnp.pad(a.astype(F32), ((0, 0), (0, npts - sig))) for a in numbers]
    exact = jnp.concatenate([coords, weights[:, None]], axis=1)
    extra = jnp.concatenate([jnp.stack(numbers, axis=1)] + thirds(exact), axis=1).astype(BF16)
    extra = jnp.pad(extra, ((0, 0), (0, EXTRA - extra.shape[1]), (0, span - npts)))
    payload = jnp.concatenate([colloc, extra], axis=1)
    near = []
    for chunk in range(2):
        part = payload[None, chunk * count : (chunk + 1) * count]
        near.append(across([(part, [0])], high_bits[::-1] if chunk else high_bits))

    payload, occupied = lax.optimization_barrier((payload, occupied))
    held, send = occupied_part(occupied, colloc, blocks, meta, blk)
    for s in range(n_ao.bit_length() - 1):
        held = held + swap(send, "ao", 1 << s).astype(F32)
        send = held.astype(BF16)
    occ = across([(send[None], [0])], high_bits)

    for bit in part_bits:
        panels = panels + [(swap(a, "grid", bit), (over, m ^ bit)) for a, (over, m) in panels]
    far = [within(pieces, low_bits) for pieces in near]

    def facts_of(pieces):
        rows = jnp.concatenate([a[:, :, npts:, :npts] for a, _ in pieces], axis=0).astype(F32)
        ids = (rows[:, :, 0, :sig] + 128 * rows[:, :, 1, :sig]).astype(jnp.int32)
        return ids, rows[:, :, 2:6] + rows[:, :, 6:10] + rows[:, :, 10:14]

    all_ids = [facts_of(pieces)[0] for pieces in far]
    facts, columns = select(far, all_ids, meta, rank, nown, npts)

    early, late = [], []
    for chunk in range(2):
        ids, exact = facts_of(near[chunk])
        kern = kernel_matrix(exact[:, :, :3], exact[:, :, 3])
        e = potential(panels, near[chunk], occ, kern, ids, meta, chunk * count, nlocal, rank)
        pieces = across([(e[None], [0])], high_bits[::-1] if chunk else high_bits)
        early += [(chunk, a, m) for a, m in within(pieces[:1], low_bits)]
        late += [(chunk, a, m) for a, m in within(pieces[1:], low_bits)]
    total = project(early, facts, columns, meta, None, rank, nown, 4 * sig)
    total = project(late, facts, columns, meta, total, rank, nown, 4 * sig)
    return total.reshape(nv, nown * blk, 2, nocc)


def solution(mesh):
    in_specs = (
        P("ao", None, None, None),
        P("ao", None, None),
        P("grid", None, None),
        P("grid", None),
        P("grid", None, None),
        P("grid", None),
    )
    out_specs = P("ao", "grid", None, None)

    return jax.shard_map(on_device, mesh=mesh, in_specs=in_specs, out_specs=out_specs, check_vma=False)
```

profile of v0, /device:TPU:25, one launch (start us, length us, event | category | flops | bytes accessed | tf_op | source)
XLA Modules:
  0.0 277.6 jit_solution(7291452519334528555)
XLA Ops:
  0.7 12.8 %pack.1 = (bf16[12,128,256]{2,1,0:T(8,128)(2,1)}, bf16[12,128,256]{2,1,0:T(8,128)(2,1)}, bf16[12,128,256]{2,1,0:T(8,128)(2,1)}, bf16[12,128,256]{2,1,0:T(8,128)(2,1)}) custom-call(s32[5]{0:T(128)} %stack.49.where, bf16[3072,16,2,128]{3,2,1,0:T(2,128)(2,1)} %trial.1), custom_call_target="tpu_custom_call" | custom-call | tf_op jit(solution)/shard_map/pack/pallas_call | solution.py:56
  14.2 1.3 collective-permute-start.4
  16.1 4.6 %occupied.1 = (f32[4,128,256]{2,1,0:T(8,128)}, bf16[4,128,256]{2,1,0:T(8,128)(2,1)}) custom-call(s32[4,12]{1,0:T(4,128)} %ids, s32[6]{0:T(128)} %stack.57.refs_2_.meta, bf16[3072,2,128]{2,1,0:T(2,128)(2,1)} %occupied.2, bf16[4,128,1536]{2,1,0:T(8,128)(2,1)} %values), custom_call_target="tpu_custom_call" | custom-call | tf_op jit(solution)/shard_map/occupied/pallas_call | solution.py:96
  22.2 12.6 %collective-permute-done.4 = bf16[1,2,144,1536]{3,2,1,0:T(8,128)(2,1)S(1)} collective-permute-done((bf16[1,2,144,1536]{3,2,1,0:T(8,128)(2,1)S(1)}, bf16[1,2,144,1536]{3,2,1,0:T(8,128)(2,1)S(1)}, u32[]{:S(2)}, u32[]{:S(2)}) %collective-permute-start.4) | collective-permute-done | bytes 884768 | tf_op jit(solution)/shard_map/ppermute | solution.py:350
  37.1 2.2 collective-permute-start.8
  39.3 29.2 %collective-permute-done.16 = bf16[4,128,256]{2,1,0:T(8,128)(2,1)S(1)} collective-permute-done((bf16[4,128,256]{2,1,0:T(8,128)(2,1)S(1)}, bf16[4,128,256]{2,1,0:T(8,128)(2,1)S(1)}, u32[]{:S(2)}, u32[]{:S(2)}) %collective-permute-start.16) | collective-permute-done | bytes 262176 | tf_op jit(solution)/shard_map/ppermute | solution.py:350
  69.2 1.3 collective-permute-start.1
  70.5 14.1 %collective-permute-done.17 = bf16[1,4,128,256]{3,2,1,0:T(8,128)(2,1)S(1)} collective-permute-done((bf16[1,4,128,256]{3,2,1,0:T(8,128)(2,1)S(1)}, bf16[1,4,128,256]{3,2,1,0:T(8,128)(2,1)S(1)}, u32[]{:S(2)}, u32[]{:S(2)}) %collective-permute-start.17) | collective-permute-done | bytes 262176 | tf_op jit(solution)/shard_map/ppermute | solution.py:350
  85.8 2.3 collective-permute-start.14
  88.2 30.9 %collective-permute-done.9.refs_1_ = bf16[12,128,256]{2,1,0:T(8,128)(2,1)S(1)} collective-permute-done((bf16[12,128,256]{2,1,0:T(8,128)(2,1)S(1)}, bf16[12,128,256]{2,1,0:T(8,128)(2,1)S(1)}, u32[]{:S(2)}, u32[]{:S(2)}) %collective-permute-start.9) | collective-permute-done | bytes 786464 | tf_op jit(solution)/shard_map/ppermute | solution.py:350
  122.8 9.3 %collective-permute-done.18.refs_11_ = bf16[2,4,128,256]{3,2,1,0:T(8,128)(2,1)S(1)} collective-permute-done((bf16[2,4,128,256]{3,2,1,0:T(8,128)(2,1)S(1)}, bf16[2,4,128,256]{3,2,1,0:T(8,128)(2,1)S(1)}, u32[]{:S(2)}, u32[]{:S(2)}) %collective-permute-start.18) | collective-permute-done | bytes 524320 | tf_op jit(solution)/shard_map/ppermute | solution.py:350
  132.1 1.4 collective-permute-start.6
  137.2 9.9 %potential.3 = bf16[4,2,128,256]{3,2,1,0:T(8,128)(2,1)} custom-call(s32[4,2,12]{2,1,0:T(2,128)} %bitcast.38, s32[6]{0:T(128)} %stack.57.refs_2_.meta, bf16[12,128,256]{2,1,0:T(8,128)(2,1)} %copy-done.9, bf16[12,128,256]{2,1,0:T(8,128)(2,1)} %copy-done.10, bf16[12,128,256]{2,1,0:T(8,128)(2,1)} %copy-done.11, bf16[12,128,256]{2,1,0:T(8,128)(2,1)} %get-tuple-element.25.refs_3_, ...), custom_call_target="tpu_custom_call" | custom-call | tf_op jit(solution)/shard_map/potential/pallas_call | solution.py:163
  147.1 1.3 collective-permute-start.22
  151.9 9.8 %potential.2 = bf16[4,2,128,256]{3,2,1,0:T(8,128)(2,1)} custom-call(s32[4,2,12]{2,1,0:T(2,128)} %bitcast.39, s32[6]{0:T(128)} %stack.57.refs_2_.meta, bf16[12,128,256]{2,1,0:T(8,128)(2,1)} %copy-done.9, bf16[12,128,256]{2,1,0:T(8,128)(2,1)} %copy-done.10, bf16[12,128,256]{2,1,0:T(8,128)(2,1)} %copy-done.11, bf16[12,128,256]{2,1,0:T(8,128)(2,1)} %get-tuple-element.25.refs_3_, ...), custom_call_target="tpu_custom_call" | custom-call | tf_op jit(solution)/shard_map/potential/pallas_call | solution.py:163
  162.0 2.1 pad_maximum_fusion.3.refs_2_
  165.4 10.1 %collective-permute-done.19 = bf16[1,4,2,128,256]{4,3,2,1,0:T(8,128)(2,1)S(1)} collective-permute-done((bf16[1,4,2,128,256]{4,3,2,1,0:T(8,128)(2,1)}, bf16[1,4,2,128,256]{4,3,2,1,0:T(8,128)(2,1)S(1)}, u32[]{:S(2)}, u32[]{:S(2)}) %collective-permute-start.19) | collective-permute-done | bytes 524320 | tf_op jit(solution)/shard_map/ppermute | solution.py:350
  176.8 1.6 collective-permute-start.3
  178.4 19.6 %collective-permute-done.23.refs_2_ = bf16[2,4,2,128,256]{4,3,2,1,0:T(8,128)(2,1)} collective-permute-done((bf16[2,4,2,128,256]{4,3,2,1,0:T(8,128)(2,1)}, bf16[2,4,2,128,256]{4,3,2,1,0:T(8,128)(2,1)}, u32[]{:S(2)}, u32[]{:S(2)}) %collective-permute-start.23) | collective-permute-done | bytes 1048608 | tf_op jit(solution)/shard_map/ppermute | solution.py:350
  198.9 1.3 collective-permute-done.20.refs_0_
  200.2 2.2 collective-permute-start.24
  205.9 22.2 %select.20 = (s32[6,384]{1,0:T(8,128)}, bf16[384,128,128]{2,1,0:T(8,128)(2,1)}) custom-call(s32[8,2,12]{2,1,0:T(2,128)} %bitcast.37, s32[8,2,12]{2,1,0:T(2,128)} %bitcast.36, s32[6]{0:T(128)} %stack.57.refs_2_.meta, bf16[2,2,144,1536]{3,2,1,0:T(8,128)(2,1)} %copy-done.1, bf16[2,2,144,1536]{3,2,1,0:T(8,128)(2,1)} %collective-permute-done.1.refs_4_.refs_9_, ...), custom_call_target="tpu_custom_call" | custom-call | tf_op jit(solution)/shard_map/select/pallas_call | solution.py:238
  229.1 22.7 %project.2.refs_4_ = f32[4,12,128,256]{3,2,1,0:T(8,128)} custom-call(s32[6,384]{1,0:T(8,128)} %get-tuple-element.20.facts, s32[6]{0:T(128)} %stack.57.refs_2_.meta, bf16[384,128,128]{2,1,0:T(8,128)(2,1)} %get-tuple-element.21.columns, bf16[2,4,2,128,256]{4,3,2,1,0:T(8,128)(2,1)} %pad_maximum_fusion.2.refs_0_, ...), custom_call_target="tpu_custom_call" | custom-call | tf_op jit(solution)/shard_map/project/pallas_call | solution.py:331
  252.8 24.7 %project.3 = f32[4,3072,128]{2,1,0:T(8,128)} custom-call(s32[6,384]{1,0:T(8,128)} %get-tuple-element.20.facts, s32[6]{0:T(128)} %stack.57.refs_2_.meta, bf16[384,128,128]{2,1,0:T(8,128)(2,1)} %get-tuple-element.21.columns, bf16[2,4,2,128,256]{4,3,2,1,0:T(8,128)(2,1)} %collective-permute-done.20.refs_0_, bf16[2,4,2,128,256]{4,3,2,1,0:T(8,128)(2,1)} %copy-done.22, ...), custom_call_target="tpu_custom_call" | custom-call | tf_op jit(solution)/shard_map/project/pallas_call | solution.py:331
  (133 shorter events, 27.4 us)
Async XLA Ops:
  14.2 20.6 %collective-permute-start.4 = (bf16[1,2,144,1536]{3,2,1,0:T(8,128)(2,1)S(1)}, bf16[1,2,144,1536]{3,2,1,0:T(8,128)(2,1)S(1)}, u32[]{:S(2)}, u32[]{:S(2)}) collective-permute-start(bf16[1,2,144,1536]{3,2,1,0:T(8,128)(2,1)S(1)} %get-tuple-element.29), channel_id=1, source_target_pairs={{0,16},{4,20},{8,24},{12,28},{16,0},{20,4},{24,8},{28,12},{1,17},{... | collective-permute-start | bytes 2654216 | tf_op jit(solution)/shard_map/ppermute | solution.py:350
  20.8 16.2 %collective-permute-start.15 = (bf16[4,128,256]{2,1,0:T(8,128)(2,1)}, bf16[4,128,256]{2,1,0:T(8,128)(2,1)S(1)}, u32[]{:S(2)}, u32[]{:S(2)}) collective-permute-start(bf16[4,128,256]{2,1,0:T(8,128)(2,1)} %get-tuple-element.28), channel_id=1, source_target_pairs={{0,1},{1,0},{2,3},{3,2},{4,5},{5,4},{6,7},{7,6},{8,9},{9,8},{10,11... | collective-permute-start | bytes 786440 | tf_op jit(solution)/shard_map/ppermute | solution.py:350
  20.9 48.1 %collective-permute-start = (bf16[1,2,144,1536]{3,2,1,0:T(8,128)(2,1)S(1)}, bf16[1,2,144,1536]{3,2,1,0:T(8,128)(2,1)S(1)}, u32[]{:S(2)}, u32[]{:S(2)}) collective-permute-start(bf16[1,2,144,1536]{3,2,1,0:T(8,128)(2,1)S(1)} %get-tuple-element.30), channel_id=1, source_target_pairs={{0,8},{4,12},{8,0},{12,4},{16,24},{20,28},{24,16},{28,20},{1,9},{5... | collective-permute-start | bytes 2654216 | tf_op jit(solution)/shard_map/ppermute | solution.py:350
  35.7 85.7 %collective-permute-start.5 = (bf16[2,2,144,1536]{3,2,1,0:T(8,128)(2,1)S(1)}, bf16[2,2,144,1536]{3,2,1,0:T(8,128)(2,1)S(1)}, u32[]{:S(2)}, u32[]{:S(2)}) collective-permute-start(bf16[2,2,144,1536]{3,2,1,0:T(8,128)(2,1)S(1)} %pad_maximum_fusion.1.refs_7_.refs_8_), channel_id=1, source_target_pairs={{0,8},{4,12},{8,0},{12,4},{16,24},{20,28},{24,16},{28,20},{1,9},{5... | collective-permute-start | bytes 5308424 | tf_op jit(solution)/shard_map/ppermute | solution.py:350
  37.0 31.6 %collective-permute-start.16 = (bf16[4,128,256]{2,1,0:T(8,128)(2,1)S(1)}, bf16[4,128,256]{2,1,0:T(8,128)(2,1)S(1)}, u32[]{:S(2)}, u32[]{:S(2)}) collective-permute-start(bf16[4,128,256]{2,1,0:T(8,128)(2,1)S(1)} %fusion.2), channel_id=1, source_target_pairs={{0,2},{1,3},{2,0},{3,1},{4,6},{5,7},{6,4},{7,5},{8,10},{9,11},{10,... | collective-permute-start | bytes 786440 | tf_op jit(solution)/shard_map/ppermute | solution.py:350
  37.1 48.7 %collective-permute-start.8 = (bf16[12,128,256]{2,1,0:T(8,128)(2,1)S(1)}, bf16[12,128,256]{2,1,0:T(8,128)(2,1)S(1)}, u32[]{:S(2)}, u32[]{:S(2)}) collective-permute-start(bf16[12,128,256]{2,1,0:T(8,128)(2,1)S(1)} %copy-done.28), channel_id=1, source_target_pairs={{0,3},{1,2},{2,1},{3,0},{4,7},{5,6},{6,5},{7,4},{8,11},{9,10},{10,... | collective-permute-start | bytes 2359304 | tf_op jit(solution)/shard_map/ppermute | solution.py:350
  68.7 15.9 %collective-permute-start.17 = (bf16[1,4,128,256]{3,2,1,0:T(8,128)(2,1)S(1)}, bf16[1,4,128,256]{3,2,1,0:T(8,128)(2,1)S(1)}, u32[]{:S(2)}, u32[]{:S(2)}) collective-permute-start(bf16[1,4,128,256]{3,2,1,0:T(8,128)(2,1)S(1)} %fusion.3), channel_id=1, source_target_pairs={{0,8},{4,12},{8,0},{12,4},{16,24},{20,28},{24,16},{28,20},{1,9},{5... | collective-permute-start | bytes 786440 | tf_op jit(solution)/shard_map/ppermute | solution.py:350
  69.2 79.3 %collective-permute-start.1 = (bf16[2,2,144,1536]{3,2,1,0:T(8,128)(2,1)S(1)}, bf16[2,2,144,1536]{3,2,1,0:T(8,128)(2,1)}, u32[]{:S(2)}, u32[]{:S(2)}) collective-permute-start(bf16[2,2,144,1536]{3,2,1,0:T(8,128)(2,1)S(1)} %pad_maximum_fusion.refs_3_.refs_8_), channel_id=1, source_target_pairs={{0,16},{4,20},{8,24},{12,28},{16,0},{20,4},{24,8},{28,12},{1,17},{... | collective-permute-start | bytes 5308424 | tf_op jit(solution)/shard_map/ppermute | solution.py:350
  70.5 48.7 %collective-permute-start.9 = (bf16[12,128,256]{2,1,0:T(8,128)(2,1)S(1)}, bf16[12,128,256]{2,1,0:T(8,128)(2,1)S(1)}, u32[]{:S(2)}, u32[]{:S(2)}) collective-permute-start(bf16[12,128,256]{2,1,0:T(8,128)(2,1)S(1)} %copy-done.27), channel_id=1, source_target_pairs={{0,2},{1,3},{2,0},{3,1},{4,6},{5,7},{6,4},{7,5},{8,10},{9,11},{10,... | collective-permute-start | bytes 2359304 | tf_op jit(solution)/shard_map/ppermute | solution.py:350
  84.6 35.9 %collective-permute-start.10 = (bf16[12,128,256]{2,1,0:T(8,128)(2,1)S(1)}, bf16[12,128,256]{2,1,0:T(8,128)(2,1)S(1)}, u32[]{:S(2)}, u32[]{:S(2)}) collective-permute-start(bf16[12,128,256]{2,1,0:T(8,128)(2,1)S(1)} %copy-done.26), channel_id=1, source_target_pairs={{0,1},{1,0},{2,3},{3,2},{4,5},{5,4},{6,7},{7,6},{8,9},{9,8},{10,11... | collective-permute-start | bytes 2359304 | tf_op jit(solution)/shard_map/ppermute | solution.py:350
  85.8 35.5 %collective-permute-start.14 = (bf16[12,128,256]{2,1,0:T(8,128)(2,1)S(1)}, bf16[12,128,256]{2,1,0:T(8,128)(2,1)S(1)}, u32[]{:S(2)}, u32[]{:S(2)}) collective-permute-start(bf16[12,128,256]{2,1,0:T(8,128)(2,1)S(1)} %copy-done.8), channel_id=1, source_target_pairs={{0,4},{4,0},{8,12},{12,8},{16,20},{20,16},{24,28},{28,24},{1,5},{5... | collective-permute-start | bytes 2359304 | tf_op jit(solution)/shard_map/ppermute | solution.py:350
  120.4 14.8 %collective-permute-start.11 = (bf16[12,128,256]{2,1,0:T(8,128)(2,1)S(1)}, bf16[12,128,256]{2,1,0:T(8,128)(2,1)S(1)}, u32[]{:S(2)}, u32[]{:S(2)}) collective-permute-start(bf16[12,128,256]{2,1,0:T(8,128)(2,1)S(1)} %collective-permute-done.8.refs_0_), channel_id=1, source_target_pairs={{0,4},{4,0},{8,12},{12,8},{16,20},{20,16},{24,28},{28,24},{1,5},{5... | collective-permute-start | bytes 2359304 | tf_op jit(solution)/shard_map/ppermute | solution.py:350
  121.4 13.9 %collective-permute-start.12 = (bf16[12,128,256]{2,1,0:T(8,128)(2,1)S(1)}, bf16[12,128,256]{2,1,0:T(8,128)(2,1)S(1)}, u32[]{:S(2)}, u32[]{:S(2)}) collective-permute-start(bf16[12,128,256]{2,1,0:T(8,128)(2,1)S(1)} %collective-permute-done.9.refs_1_), channel_id=1, source_target_pairs={{0,4},{4,0},{8,12},{12,8},{16,20},{20,16},{24,28},{28,24},{1,5},{5... | collective-permute-start | bytes 2359304 | tf_op jit(solution)/shard_map/ppermute | solution.py:350
  132.1 44.7 %collective-permute-start.6 = (bf16[2,2,144,1536]{3,2,1,0:T(8,128)(2,1)S(1)}, bf16[2,2,144,1536]{3,2,1,0:T(8,128)(2,1)}, u32[]{:S(2)}, u32[]{:S(2)}) collective-permute-start(bf16[2,2,144,1536]{3,2,1,0:T(8,128)(2,1)S(1)} %pad_maximum_fusion.1.refs_7_.refs_8_), channel_id=1, source_target_pairs={{0,4},{4,0},{8,12},{12,8},{16,20},{20,16},{24,28},{28,24},{1,5},{5... | collective-permute-start | bytes 5308424 | tf_op jit(solution)/shard_map/ppermute | solution.py:350
  135.2 43.2 %collective-permute-start.2 = (bf16[2,2,144,1536]{3,2,1,0:T(8,128)(2,1)S(1)}, bf16[2,2,144,1536]{3,2,1,0:T(8,128)(2,1)}, u32[]{:S(2)}, u32[]{:S(2)}) collective-permute-start(bf16[2,2,144,1536]{3,2,1,0:T(8,128)(2,1)S(1)} %pad_maximum_fusion.refs_3_.refs_8_), channel_id=1, source_target_pairs={{0,4},{4,0},{8,12},{12,8},{16,20},{20,16},{24,28},{28,24},{1,5},{5... | collective-permute-start | bytes 5308424 | tf_op jit(solution)/shard_map/ppermute | solution.py:350
  147.1 14.9 %collective-permute-start.22 = (bf16[1,4,2,128,256]{4,3,2,1,0:T(8,128)(2,1)}, bf16[1,4,2,128,256]{4,3,2,1,0:T(8,128)(2,1)}, u32[]{:S(2)}, u32[]{:S(2)}) collective-permute-start(bf16[1,4,2,128,256]{4,3,2,1,0:T(8,128)(2,1)} %bitcast.30), channel_id=1, source_target_pairs={{0,16},{4,20},{8,24},{12,28},{16,0},{20,4},{24,8},{28,12},{1,17},{... | collective-permute-start | bytes 1572872 | tf_op jit(solution)/shard_map/ppermute | solution.py:350
  150.7 51.7 %collective-permute-start.7 = (bf16[2,2,144,1536]{3,2,1,0:T(8,128)(2,1)S(1)}, bf16[2,2,144,1536]{3,2,1,0:T(8,128)(2,1)}, u32[]{:S(2)}, u32[]{:S(2)}) collective-permute-start(bf16[2,2,144,1536]{3,2,1,0:T(8,128)(2,1)S(1)} %copy-done.3), channel_id=1, source_target_pairs={{0,4},{4,0},{8,12},{12,8},{16,20},{20,16},{24,28},{28,24},{1,5},{5... | collective-permute-start | bytes 5308424 | tf_op jit(solution)/shard_map/ppermute | solution.py:350
  164.1 33.9 %collective-permute-start.23 = (bf16[2,4,2,128,256]{4,3,2,1,0:T(8,128)(2,1)}, bf16[2,4,2,128,256]{4,3,2,1,0:T(8,128)(2,1)}, u32[]{:S(2)}, u32[]{:S(2)}) collective-permute-start(bf16[2,4,2,128,256]{4,3,2,1,0:T(8,128)(2,1)} %pad_maximum_fusion.3.refs_2_), channel_id=1, source_target_pairs={{0,8},{4,12},{8,0},{12,4},{16,24},{20,28},{24,16},{28,20},{1,9},{5... | collective-permute-start | bytes 3145736 | tf_op jit(solution)/shard_map/ppermute | solution.py:350
  176.5 23.7 %collective-permute-start.20 = (bf16[2,4,2,128,256]{4,3,2,1,0:T(8,128)(2,1)}, bf16[2,4,2,128,256]{4,3,2,1,0:T(8,128)(2,1)}, u32[]{:S(2)}, u32[]{:S(2)}) collective-permute-start(bf16[2,4,2,128,256]{4,3,2,1,0:T(8,128)(2,1)} %pad_maximum_fusion.2.refs_0_), channel_id=1, source_target_pairs={{0,16},{4,20},{8,24},{12,28},{16,0},{20,4},{24,8},{28,12},{1,17},{... | collective-permute-start | bytes 3145736 | tf_op jit(solution)/shard_map/ppermute | solution.py:350
  176.8 27.8 %collective-permute-start.3 = (bf16[2,2,144,1536]{3,2,1,0:T(8,128)(2,1)}, bf16[2,2,144,1536]{3,2,1,0:T(8,128)(2,1)S(1)}, u32[]{:S(2)}, u32[]{:S(2)}) collective-permute-start(bf16[2,2,144,1536]{3,2,1,0:T(8,128)(2,1)} %collective-permute-done.1.refs_4_.refs_9_), channel_id=1, source_target_pairs={{0,4},{4,0},{8,12},{12,8},{16,20},{20,16},{24,28},{28,24},{1,5},{5... | collective-permute-start | bytes 5308424 | tf_op jit(solution)/shard_map/ppermute | solution.py:350
  178.4 49.7 %collective-permute-start.26 = (bf16[2,4,2,128,256]{4,3,2,1,0:T(8,128)(2,1)}, bf16[2,4,2,128,256]{4,3,2,1,0:T(8,128)(2,1)S(1)}, u32[]{:S(2)}, u32[]{:S(2)}) collective-permute-start(bf16[2,4,2,128,256]{4,3,2,1,0:T(8,128)(2,1)} %pad_maximum_fusion.3.refs_2_), channel_id=1, source_target_pairs={{0,4},{4,0},{8,12},{12,8},{16,20},{20,16},{24,28},{28,24},{1,5},{5... | collective-permute-start | bytes 3145736 | tf_op jit(solution)/shard_map/ppermute | solution.py:350
  198.0 30.1 %collective-permute-start.25 = (bf16[2,4,2,128,256]{4,3,2,1,0:T(8,128)(2,1)}, bf16[2,4,2,128,256]{4,3,2,1,0:T(8,128)(2,1)}, u32[]{:S(2)}, u32[]{:S(2)}) collective-permute-start(bf16[2,4,2,128,256]{4,3,2,1,0:T(8,128)(2,1)} %pad_maximum_fusion.2.refs_0_), channel_id=1, source_target_pairs={{0,4},{4,0},{8,12},{12,8},{16,20},{20,16},{24,28},{28,24},{1,5},{5... | collective-permute-start | bytes 3145736 | tf_op jit(solution)/shard_map/ppermute | solution.py:350
  200.2 51.6 %collective-permute-start.24 = (bf16[2,4,2,128,256]{4,3,2,1,0:T(8,128)(2,1)}, bf16[2,4,2,128,256]{4,3,2,1,0:T(8,128)(2,1)}, u32[]{:S(2)}, u32[]{:S(2)}) collective-permute-start(bf16[2,4,2,128,256]{4,3,2,1,0:T(8,128)(2,1)} %collective-permute-done.23.refs_2_), channel_id=1, source_target_pairs={{0,4},{4,0},{8,12},{12,8},{16,20},{20,16},{24,28},{28,24},{1,5},{5... | collective-permute-start | bytes 3145736 | tf_op jit(solution)/shard_map/ppermute | solution.py:350
  202.4 49.4 %collective-permute-start.21 = (bf16[2,4,2,128,256]{4,3,2,1,0:T(8,128)(2,1)}, bf16[2,4,2,128,256]{4,3,2,1,0:T(8,128)(2,1)S(1)}, u32[]{:S(2)}, u32[]{:S(2)}) collective-permute-start(bf16[2,4,2,128,256]{4,3,2,1,0:T(8,128)(2,1)} %collective-permute-done.20.refs_0_), channel_id=1, source_target_pairs={{0,4},{4,0},{8,12},{12,8},{16,20},{20,16},{24,28},{28,24},{1,5},{5... | collective-permute-start | bytes 3145736 | tf_op jit(solution)/shard_map/ppermute | solution.py:350
  (32 other events, 523.3 us)
where the time goes:
time: 278 us
  waiting for transfers between devices  127 us (46%)
  Pallas kernels  107 us (38%)
  starting transfers between devices  24 us (9%)
  local copies, waits for them, and re-layouts  9.65 us (3%)
  other arithmetic  9.44 us (3%)
    ppermute x27, waiting for transfers between devices, swap(): return lax.ppermute(array, axis, [(i, i ^ bit) for i in range(size)])  127 us
    pallas_call x2, Pallas kernels, project(): pl.pallas_call(functools.partial(project_kernel, (nchunk, emasks, rank, g...  47.4 us
    ppermute x27, starting transfers between devices, swap(): return lax.ppermute(array, axis, [(i, i ^ bit) for i in range(size)])  24 us
    pallas_call x1, Pallas kernels, select(): pl.pallas_call(functools.partial(select_kernel, sizes), out_shape=(jax.Sh...  22.2 us
    pallas_call x2, Pallas kernels, potential(): pl.pallas_call(functools.partial(potential_kernel, sizes), out_shape=jax....  19.7 us
    pallas_call x1, Pallas kernels, pack(): pl.pallas_call(pack_kernel, out_shape=(jax.ShapeDtypeStruct((nb, blk, 2 *...  12.8 us
  transfers between devices with their start and end apart: 27, of which 8 were waited for; matrix products, arithmetic and copies ran while one was open for 5% of the time, Pallas kernels for 25%

commit v1 on v0

--- a/solution.py
+++ b/solution.py
@@ -41,14 +41,18 @@
             )
     for c in copies:
         c.start()
-    pick = selectors(blk)
+    pick = jnp.concatenate(selectors(blk), axis=0)
     for i, out in enumerate(outs):
-        for j in range(nb):
-            copies[i * nb + j].wait()
-            both = rows[i, j].reshape(2 * blk, nocc)
-            for c in range(2):
-                split = jnp.dot(pick[c], both, preferred_element_type=F32)
-                out[j, :, c * nocc : (c + 1) * nocc] = split.astype(BF16)
+        for j in range(0, nb, 2):
+            ahead = range(j, min(j + 2, nb))
+            for k in ahead:
+                copies[i * nb + k].wait()
+            both = jnp.concatenate([rows[i, k].reshape(2 * blk, nocc) for k in ahead], axis=1)
+            split = jnp.dot(pick, both, preferred_element_type=F32).astype(BF16)
+            for k in ahead:
+                for c in range(2):
+                    piece = split[c * blk : (c + 1) * blk, (k - j) * nocc : (k - j + 1) * nocc]
+                    out[k, :, c * nocc : (c + 1) * nocc] = piece
 
 
 def pack(trial, where, planes, nb, blk):
@@ -109,7 +113,7 @@
     panels, refs = refs[:nt], refs[nt:]
     values, refs = refs[:npiece], refs[npiece:]
     occ, refs = refs[:no], refs[no:]
-    kern, out, table, x, sems = refs
+    kern, out, table, x, left, m, sems = refs
     nb, blk, width = panels[0].shape
     nocc = width // 2
     npts = x.shape[2]
@@ -133,21 +137,26 @@
     sources = [m for masks in xmasks for m in masks]
     where = {m: (i, j) for i, masks in enumerate(omasks) for j, m in enumerate(masks)}
     dims = (((1,), (1,)), ((), ()))
-    for p, mask in enumerate(sources):
+    todo = [(p, mask, b) for p, mask in enumerate(sources) for b in range(count)]
+
+    def turn_of(mask, b):
         piece, row = where[mask]
-        for b in range(count):
-            dens = jnp.zeros((npts, width), F32)
-            for s in range(0, sig, 2):
-                panel = jnp.concatenate([table[ids[p, b, s]], table[ids[p, b, s + 1]]], axis=0)
-                dens += jnp.dot(x[p, b, :, s * blk : (s + 2) * blk], panel, preferred_element_type=F32)
-            left = dens.astype(BF16)
-            og = occ[piece][row, first + b]
-            oreal, oimag = og[:, :nocc], og[:, nocc:]
-            turn = jnp.concatenate([og, jnp.concatenate([-oimag, oreal], axis=1)], axis=0)
-            rho = lax.dot_general(left, turn, dims, preferred_element_type=F32)
-            weight = kern[p, b]
-            m = (rho * jnp.concatenate([weight, weight], axis=1)).astype(BF16)
-            out[meta[5] ^ (mask // rank), b] = jnp.dot(m, turn, preferred_element_type=F32).astype(BF16)
+        og = occ[piece][row, first + b]
+        return jnp.concatenate([og, jnp.concatenate([-og[:, nocc:], og[:, :nocc]], axis=1)], axis=0)
+
+    for i, (p, mask, b) in enumerate(todo):
+        dens = jnp.zeros((npts, width), F32)
+        for s in range(0, sig, 2):
+            panel = jnp.concatenate([table[ids[p, b, s]], table[ids[p, b, s + 1]]], axis=0)
+            dens += jnp.dot(x[p, b, :, s * blk : (s + 2) * blk], panel, preferred_element_type=F32)
+        left[i] = dens.astype(BF16)
+    for i, (p, mask, b) in enumerate(todo):
+        rho = lax.dot_general(left[i], turn_of(mask, b), dims, preferred_element_type=F32)
+        weight = kern[p, b]
+        m[i] = (rho * jnp.concatenate([weight, weight], axis=1)).astype(BF16)
+    for i, (p, mask, b) in enumerate(todo):
+        e = jnp.dot(m[i], turn_of(mask, b), preferred_element_type=F32)
+        out[meta[5] ^ (mask // rank), b] = e.astype(BF16)
 
 
 def potential(panels, values, occ, kern, ids, meta, first, nlocal, rank):
@@ -168,6 +177,8 @@
         scratch_shapes=[
             pltpu.VMEM((total, blk, width), BF16),
             pltpu.VMEM((nsrc, count, npts, sig * blk), BF16),
+            pltpu.VMEM((nsrc * count, npts, width), BF16),
+            pltpu.VMEM((nsrc * count, npts, 2 * npts), BF16),
             pltpu.SemaphoreType.DMA((nt + npiece,)),
         ],
         compiler_params=PARAMS,
@@ -176,73 +187,112 @@
 
 
 def select_kernel(sizes, *refs):
-    ncall, xmasks, rank, nown = sizes
+    ncall, xmasks, rank, nown, group = sizes
     all_ids, refs = refs[:ncall], refs[ncall:]
     meta, refs = refs[0], refs[1:]
-    flat = [m for masks in xmasks for m in masks]
-    values, (facts, columns, x, sems) = refs[: len(flat)], refs[len(flat) :]
-    ncount = all_ids[0].shape[1]
+    values, (facts, columns, x, rows, place, xsems, osems) = refs[: len(xmasks)], refs[len(xmasks) :]
     sig = all_ids[0].shape[2]
     npts = x.shape[2]
     blk = x.shape[3] // sig
     copies = []
-    place = 0
-    starts = []
+    at = 0
+    entries = []
+    groups = len(values) // ncall
     for i, piece in enumerate(values):
         size = piece.shape[0]
-        copies.append(pltpu.make_async_copy(piece.at[:, :, pl.ds(0, npts)], x.at[pl.ds(place, size)], sems.at[i]))
-        starts.append(place)
-        place += size
+        copies.append(pltpu.make_async_copy(piece.at[:, :, pl.ds(0, npts)], x.at[pl.ds(at, size)], xsems.at[i]))
+        if i % groups == 0:
+            p = 0
+        for j, mask in enumerate(xmasks[i]):
+            entries += [(i // groups, p, mask, b, at + j) for b in range(x.shape[1])]
+            p += 1
+        at += size
     for c in copies:
         c.start()
+    nlist = nown * ncall
+    for o in range(nlist + 1):
+        place[o] = 0
+
+    def slot(chunk, p, b, s):
+        own = all_ids[chunk][p, b, s] - meta[2]
+        return jnp.where((own >= 0) & (own < nown), own * ncall + chunk, nlist)
+
+    def blank(at, own, chunk):
+        facts[0, at] = own
+        facts[1, at] = chunk
+        for f in range(2, 5):
+            facts[f, at] = 0
+        rows[at] = jnp.zeros(rows.shape[1:], BF16)
+
+    for chunk, p, _, b, _ in entries:
+        for s in range(sig):
+            own = slot(chunk, p, b, s)
+            place[own] = place[own] + 1
+    n = jnp.int32(0)
+    for o in range(nlist):
+        size = place[o]
+        place[o] = n
+        odd = lax.rem(size, 2)
+
+        @pl.when(odd == 1)
+        def _(at=n + size, o=o):
+            blank(at, o // ncall, o % ncall)
+
+        n = n + size + odd
+    blank(n, 0, 0)
+    blank(n + 1, 0, 0)
+    n = n + lax.rem(n, 4)
+    facts[5, 0] = n
     for c in copies:
         c.wait()
-    n = jnp.int32(0)
-    place = 0
-    groups = len(values) // ncall
-    for chunk in range(ncall):
-        p = 0
-        for i in range(groups):
-            piece = chunk * groups + i
-            for j, mask in enumerate(flat[piece]):
-                for b in range(ncount):
-
-                    def one(s, n, chunk=chunk, p=p, mask=mask, b=b, row=starts[piece] + j):
-                        own = all_ids[chunk][p, b, s] - meta[2]
-                        mine = (own >= 0) & (own < nown)
-
-                        @pl.when(mine)
-                        def _():
-                            facts[0, n] = own
-                            facts[1, n] = chunk
-                            facts[2, n] = mask % rank
-                            facts[3, n] = meta[5] ^ (mask // rank)
-                            facts[4, n] = b
-                            at = pl.multiple_of(s * blk, blk)
-                            columns[n] = x[row, b, :, pl.ds(at, blk)].T
-
-                        return n + mine.astype(jnp.int32)
-
-                    n = lax.fori_loop(0, sig, one, n)
-                p += 1
-    facts[5, 0] = n
-
-
-def select(values, all_ids, meta, rank, nown, npts):
+    for chunk, p, mask, b, row in entries:
+
+        def one(s, carry, chunk=chunk, p=p, mask=mask, b=b, row=row):
+            own = slot(chunk, p, b, s)
+
+            @pl.when(own < nlist)
+            def _():
+                to = place[own]
+                place[own] = to + 1
+                facts[0, to] = lax.div(own, ncall)
+                facts[1, to] = chunk
+                facts[2, to] = mask % rank
+                facts[3, to] = meta[5] ^ (mask // rank)
+                facts[4, to] = b
+                rows[to] = x[row, b, :, pl.ds(pl.multiple_of(s * blk, blk), blk)].T
+
+            return carry
+
+        lax.fori_loop(0, sig, one, 0)
+    outs = [
+        pltpu.make_async_copy(rows.at[pl.ds(i * group, group)], columns.at[pl.ds(i * group, group)], osems.at[i])
+        for i in range(columns.shape[0] // group)
+    ]
+    for act in ("start", "wait"):
+        for i, c in enumerate(outs):
+
+            @pl.when(i * group < n)
+            def _(c=c, act=act):
+                getattr(c, act)()
+
+
+def select(values, all_ids, meta, rank, nown, npts, group):
     flat = [piece for pieces in values for piece in pieces]
-    xmasks = tuple((tuple(m),) for _, m in flat)
+    xmasks = tuple(tuple(m) for _, m in flat)
     nsrc, count, sig = all_ids[0].shape
     blk = flat[0][0].shape[-1] // sig
-    most = len(values) * nsrc * count * sig
-    sizes = (len(values), tuple(tuple(m) for m in xmasks), rank, nown)
+    most = -(-(len(values) * (nsrc * count * sig + nown) + 4) // group) * group
     return pl.pallas_call(
-        functools.partial(select_kernel, sizes),
+        functools.partial(select_kernel, (len(values), xmasks, rank, nown, group)),
         out_shape=(jax.ShapeDtypeStruct((6, most), jnp.int32), jax.ShapeDtypeStruct((most, blk, npts), BF16)),
         in_specs=[SMEM] * (len(values) + 1) + [ANY] * len(flat),
-        out_specs=(SMEM, VMEM),
+        out_specs=(SMEM, ANY),
         scratch_shapes=[
             pltpu.VMEM((len(values) * nsrc, count, npts, sig * blk), BF16),
+            pltpu.VMEM((most, blk, npts), BF16),
+            pltpu.SMEM((nown * len(values) + 1,), jnp.int32),
             pltpu.SemaphoreType.DMA((len(flat),)),
+            pltpu.SemaphoreType.DMA((most // group,)),
         ],
         compiler_params=PARAMS,
         name="select",
@@ -254,12 +304,11 @@
     ne = len(emasks)
     potentials, refs = refs[:ne], refs[ne:]
     before = refs[0] if last else None
-    out, x, e, acc, esems, xsems = refs[last:]
+    out, x, e, held, esems, xsems = refs[last:]
     nvs = e.shape[2]
     blk = x.shape[1]
-    nown = acc.shape[1]
+    nown = held.shape[1] if last else out.shape[1]
     n = facts[5, 0]
-    ncopy = columns.shape[0] // group
     ecopies = []
     place = {}
     for i in range(ne):
@@ -273,10 +322,10 @@
             )
             k.append(mask // rank)
     if last:
-        ecopies.append(pltpu.make_async_copy(before, acc, esems.at[len(ecopies)]))
+        ecopies.append(pltpu.make_async_copy(before, held, esems.at[len(ecopies)]))
     xcopies = [
         pltpu.make_async_copy(columns.at[pl.ds(i * group, group)], x.at[pl.ds(i * group, group)], xsems.at[i])
-        for i in range(ncopy)
+        for i in range(columns.shape[0] // group)
     ]
     for i, c in enumerate(xcopies):
 
@@ -286,8 +335,9 @@
 
     for c in ecopies:
         c.start()
+    total = held if last else out
     if not last:
-        acc[...] = jnp.zeros_like(acc)
+        total[...] = jnp.zeros_like(total)
     for i, c in enumerate(xcopies):
 
         @pl.when(i * group < n)
@@ -297,25 +347,29 @@
     for c in ecopies:
         c.wait()
 
-    def one(i, carry):
-        own, chunk, side, source, b = [facts[f, i] for f in range(5)]
+    def add(at):
+        own, chunk = facts[0, at], facts[1, at]
+        here = [[facts[f, at + t] for f in range(2, 5)] for t in range(2)]
+        left = jnp.concatenate([x[at], x[at + 1]], axis=1)
         for k in range(nvs):
             off = jnp.int32(place[(0, 0)][k])
             for other in range(1, nchunk):
                 off = jnp.where(chunk == other, place[(other, 0)][k], off)
-            vec = meta[5] ^ off
-            acc[vec, own] += jnp.dot(x[i], e[chunk, side, k, source, b], preferred_element_type=F32)
+            right = jnp.concatenate([e[chunk, side, k, source, b] for side, source, b in here], axis=0)
+            total[meta[5] ^ off, own] += jnp.dot(left, right, preferred_element_type=F32)
+
+    def one(i, carry):
+        add(4 * i)
+        add(4 * i + 2)
         return carry
 
-    lax.fori_loop(0, n, one, 0)
+    lax.fori_loop(0, lax.div(n, 4), one, 0)
     if last:
         nocc = out.shape[2]
         for v in range(out.shape[0]):
             for o in range(nown):
                 for c in range(2):
-                    out[v, pl.ds(o * 2 * blk + c, blk, stride=2), :] = acc[v, o, :, c * nocc : (c + 1) * nocc]
-    else:
-        out[...] = acc[...]
+                    out[v, pl.ds(o * 2 * blk + c, blk, stride=2), :] = total[v, o, :, c * nocc : (c + 1) * nocc]
 
 
 def project(potentials, facts, columns, meta, before, rank, nown, group):
@@ -336,7 +390,7 @@
         scratch_shapes=[
             pltpu.VMEM(columns.shape, BF16),
             pltpu.VMEM((nchunk, rank, slots, nv, count, npts, width), BF16),
-            pltpu.VMEM((nv, nown, blk, width), F32),
+            pltpu.VMEM((nv, nown, blk, width) if last else (8, 128), F32),
             pltpu.SemaphoreType.DMA((sum(len(m) for _, m in emasks) + 1,)),
             pltpu.SemaphoreType.DMA((columns.shape[0] // group,)),
         ],
@@ -401,10 +455,9 @@
     panels = []
     for over, one in zip(planes, rows, strict=True):
         panels.append((swap(one, "ao", over) if over else one, (over, 0)))
-    own = panels[-1][0]
-
-    own, colloc, blocks = lax.optimization_barrier((own, colloc, blocks))
+    own, occupied, colloc, blocks = lax.optimization_barrier((panels[-1][0], occupied, colloc, blocks))
     panels[-1] = (own, panels[-1][1])
+
     numbers = [blocks % 128, blocks // 128]
     numbers = [jnp.pad(a.astype(F32), ((0, 0), (0, npts - sig))) for a in numbers]
     exact = jnp.concatenate([coords, weights[:, None]], axis=1)
@@ -416,7 +469,6 @@
         part = payload[None, chunk * count : (chunk + 1) * count]
         near.append(across([(part, [0])], high_bits[::-1] if chunk else high_bits))
 
-    payload, occupied = lax.optimization_barrier((payload, occupied))
     held, send = occupied_part(occupied, colloc, blocks, meta, blk)
     for s in range(n_ao.bit_length() - 1):
         held = held + swap(send, "ao", 1 << s).astype(F32)
@@ -431,9 +483,6 @@
         rows = jnp.concatenate([a[:, :, npts:, :npts] for a, _ in pieces], axis=0).astype(F32)
         ids = (rows[:, :, 0, :sig] + 128 * rows[:, :, 1, :sig]).astype(jnp.int32)
         return ids, rows[:, :, 2:6] + rows[:, :, 6:10] + rows[:, :, 10:14]
-
-    all_ids = [facts_of(pieces)[0] for pieces in far]
-    facts, columns = select(far, all_ids, meta, rank, nown, npts)
 
     early, late = [], []
     for chunk in range(2):
@@ -443,8 +492,11 @@
         pieces = across([(e[None], [0])], high_bits[::-1] if chunk else high_bits)
         early += [(chunk, a, m) for a, m in within(pieces[:1], low_bits)]
         late += [(chunk, a, m) for a, m in within(pieces[1:], low_bits)]
-    total = project(early, facts, columns, meta, None, rank, nown, 4 * sig)
-    total = project(late, facts, columns, meta, total, rank, nown, 4 * sig)
+    group = 4 * sig
+    all_ids = [facts_of(pieces)[0] for pieces in far]
+    facts, columns = select(far, all_ids, meta, rank, nown, npts, group)
+    total = project(early, facts, columns, meta, None, rank, nown, group)
+    total = project(late, facts, columns, meta, total, rank, nown, group)
     return total.reshape(nv, nown * blk, 2, nocc)
 
 

time: 278 us -> 249 us (0.90)
  Pallas kernels: 107 us -> 77.1 us
  starting transfers between devices: 24 us -> 20.9 us
    pallas_call x2, Pallas kernels: 47.4 us -> 27.5 us  [project(): pl.pallas_call(functools.partial(project_kernel, (nchunk, emasks, rank, g...]
    pallas_call x2, Pallas kernels: 19.7 us -> 15.2 us  [potential(): pl.pallas_call(functools.partial(potential_kernel, sizes), out_shape=jax....]
    pallas_call x1, Pallas kernels: 12.8 us -> 9.41 us  [pack(): pl.pallas_call(pack_kernel, out_shape=(jax.ShapeDtypeStruct((nb, blk, 2 *...]
    ppermute x27, starting transfers between devices: 24 us -> 20.9 us  [swap(): return lax.ppermute(array, axis, [(i, i ^ bit) for i in range(size)])]
  transfers between devices with their start and end apart: 27 -> 27, of which waited for: 8 -> 9; matrix products, arithmetic and copies ran while one was open for 5% -> 6% of each run, Pallas kernels for 25% -> 21%
where the time goes in v1:
time: 249 us; the launch traced here: 248 us
  waiting for transfers between devices  128 us (51%)
  Pallas kernels  77.1 us (31%)
  starting transfers between devices  20.9 us (8%)
  other arithmetic  11.7 us (5%)
  local copies, waits for them, and re-layouts  9.47 us (4%)
    ppermute x27, waiting for transfers between devices, swap(): return lax.ppermute(array, axis, [(i, i ^ bit) for i in range(size)])  128 us
    pallas_call x2, Pallas kernels, project(): pl.pallas_call(functools.partial(project_kernel, (nchunk, emasks, rank, g...  27.5 us
    ppermute x27, starting transfers between devices, swap(): return lax.ppermute(array, axis, [(i, i ^ bit) for i in range(size)])  20.9 us
    pallas_call x1, Pallas kernels, select(): pl.pallas_call(functools.partial(select_kernel, (len(values), xmasks, ran...  20.3 us
    pallas_call x2, Pallas kernels, potential(): pl.pallas_call(functools.partial(potential_kernel, sizes), out_shape=jax....  15.2 us
    pallas_call x1, Pallas kernels, pack(): pl.pallas_call(pack_kernel, out_shape=(jax.ShapeDtypeStruct((nb, blk, 2 *...  9.41 us
    concatenate x7, other arithmetic, across(): jnp.concatenate([a, b], axis=0)  5.55 us
  transfers between devices with their start and end apart: 27, of which 9 were waited for; matrix products, arithmetic and copies ran while one was open for 6% of the time, Pallas kernels for 21%

profile of v1, /device:TPU:25, one launch (start us, length us, event | category | flops | bytes accessed | tf_op | source)
XLA Modules:
  0.0 248.2 jit_solution(8930018447001448461)
XLA Ops:
  0.7 9.4 %pack.1 = (bf16[12,128,256]{2,1,0:T(8,128)(2,1)}, bf16[12,128,256]{2,1,0:T(8,128)(2,1)}, bf16[12,128,256]{2,1,0:T(8,128)(2,1)}, bf16[12,128,256]{2,1,0:T(8,128)(2,1)}) custom-call(s32[5]{0:T(128)} %stack.49.where, bf16[3072,16,2,128]{3,2,1,0:T(2,128)(2,1)} %trial.1), custom_call_target="tpu_custom_call" | custom-call | tf_op jit(solution)/shard_map/pack/pallas_call | solution.py:60
  10.8 1.3 collective-permute-start
  14.0 4.6 %occupied.1 = (f32[4,128,256]{2,1,0:T(8,128)}, bf16[4,128,256]{2,1,0:T(8,128)(2,1)}) custom-call(s32[4,12]{1,0:T(4,128)} %ids, s32[6]{0:T(128)} %stack.57.refs_2_.meta, bf16[3072,2,128]{2,1,0:T(2,128)(2,1)} %occupied.2, bf16[4,128,1536]{2,1,0:T(8,128)(2,1)} %values), custom_call_target="tpu_custom_call" | custom-call | tf_op jit(solution)/shard_map/occupied/pallas_call | solution.py:100
  18.8 12.7 %collective-permute-done = bf16[1,2,144,1536]{3,2,1,0:T(8,128)(2,1)} collective-permute-done((bf16[1,2,144,1536]{3,2,1,0:T(8,128)(2,1)S(1)}, bf16[1,2,144,1536]{3,2,1,0:T(8,128)(2,1)}, u32[]{:S(2)}, u32[]{:S(2)}) %collective-permute-start) | collective-permute-done | bytes 884768 | tf_op jit(solution)/shard_map/ppermute | solution.py:404
  31.5 1.3 pad_maximum_fusion.refs_3_.refs_8_
  32.9 1.3 collective-permute-start.1
  34.4 2.2 collective-permute-start.8
  36.6 29.2 %collective-permute-done.16 = bf16[4,128,256]{2,1,0:T(8,128)(2,1)S(1)} collective-permute-done((bf16[4,128,256]{2,1,0:T(8,128)(2,1)S(1)}, bf16[4,128,256]{2,1,0:T(8,128)(2,1)S(1)}, u32[]{:S(2)}, u32[]{:S(2)}) %collective-permute-start.16) | collective-permute-done | bytes 262176 | tf_op jit(solution)/shard_map/ppermute | solution.py:404
  68.4 4.9 %collective-permute-done.17 = bf16[1,4,128,256]{3,2,1,0:T(8,128)(2,1)S(1)} collective-permute-done((bf16[1,4,128,256]{3,2,1,0:T(8,128)(2,1)S(1)}, bf16[1,4,128,256]{3,2,1,0:T(8,128)(2,1)S(1)}, u32[]{:S(2)}, u32[]{:S(2)}) %collective-permute-start.17) | collective-permute-done | bytes 262176 | tf_op jit(solution)/shard_map/ppermute | solution.py:404
  73.3 2.6 %collective-permute-start.14 = (bf16[12,128,256]{2,1,0:T(8,128)(2,1)S(1)}, bf16[12,128,256]{2,1,0:T(8,128)(2,1)S(1)}, u32[]{:S(2)}, u32[]{:S(2)}) collective-permute-start(bf16[12,128,256]{2,1,0:T(8,128)(2,1)S(1)} %copy-done.8), channel_id=1, source_target_pairs={{0,4},{4,0},{8,12},{12,8},{16,20},{20,16},{24,28},{28,24},{1,5},{5... | collective-permute-start | bytes 2359304 | tf_op jit(solution)/shard_map/ppermute | solution.py:404
  76.0 40.4 %collective-permute-done.9.refs_1_ = bf16[12,128,256]{2,1,0:T(8,128)(2,1)S(1)} collective-permute-done((bf16[12,128,256]{2,1,0:T(8,128)(2,1)S(1)}, bf16[12,128,256]{2,1,0:T(8,128)(2,1)S(1)}, u32[]{:S(2)}, u32[]{:S(2)}) %collective-permute-start.9) | collective-permute-done | bytes 786464 | tf_op jit(solution)/shard_map/ppermute | solution.py:404
  120.1 9.3 %collective-permute-done.18.refs_11_ = bf16[2,4,128,256]{3,2,1,0:T(8,128)(2,1)S(1)} collective-permute-done((bf16[2,4,128,256]{3,2,1,0:T(8,128)(2,1)S(1)}, bf16[2,4,128,256]{3,2,1,0:T(8,128)(2,1)S(1)}, u32[]{:S(2)}, u32[]{:S(2)}) %collective-permute-start.18) | collective-permute-done | bytes 524320 | tf_op jit(solution)/shard_map/ppermute | solution.py:404
  129.4 1.4 collective-permute-start.2
  133.8 7.7 %potential.2 = bf16[4,2,128,256]{3,2,1,0:T(8,128)(2,1)} custom-call(s32[4,2,12]{2,1,0:T(2,128)} %bitcast.38, s32[6]{0:T(128)} %stack.57.refs_2_.meta, bf16[12,128,256]{2,1,0:T(8,128)(2,1)} %copy-done.9, bf16[12,128,256]{2,1,0:T(8,128)(2,1)} %copy-done.10, bf16[12,128,256]{2,1,0:T(8,128)(2,1)} %copy-done.11, bf16[12,128,256]{2,1,0:T(8,128)(2,1)} %get-tuple-element.25.refs_3_, ...), custom_call_target="tpu_custom_call" | custom-call | tf_op jit(solution)/shard_map/potential/pallas_call | solution.py:172
  146.2 7.6 %potential.3 = bf16[4,2,128,256]{3,2,1,0:T(8,128)(2,1)} custom-call(s32[4,2,12]{2,1,0:T(2,128)} %bitcast.39, s32[6]{0:T(128)} %stack.57.refs_2_.meta, bf16[12,128,256]{2,1,0:T(8,128)(2,1)} %copy-done.9, bf16[12,128,256]{2,1,0:T(8,128)(2,1)} %copy-done.10, bf16[12,128,256]{2,1,0:T(8,128)(2,1)} %copy-done.11, bf16[12,128,256]{2,1,0:T(8,128)(2,1)} %get-tuple-element.25.refs_3_, ...), custom_call_target="tpu_custom_call" | custom-call | tf_op jit(solution)/shard_map/potential/pallas_call | solution.py:172
  155.0 2.2 pad_maximum_fusion.2.refs_0_
  157.6 10.0 %collective-permute-done.22 = bf16[1,4,2,128,256]{4,3,2,1,0:T(8,128)(2,1)S(1)} collective-permute-done((bf16[1,4,2,128,256]{4,3,2,1,0:T(8,128)(2,1)}, bf16[1,4,2,128,256]{4,3,2,1,0:T(8,128)(2,1)S(1)}, u32[]{:S(2)}, u32[]{:S(2)}) %collective-permute-start.22) | collective-permute-done | bytes 524320 | tf_op jit(solution)/shard_map/ppermute | solution.py:404
  168.9 1.6 collective-permute-start.7
  170.6 19.6 %collective-permute-done.20.refs_0_ = bf16[2,4,2,128,256]{4,3,2,1,0:T(8,128)(2,1)} collective-permute-done((bf16[2,4,2,128,256]{4,3,2,1,0:T(8,128)(2,1)}, bf16[2,4,2,128,256]{4,3,2,1,0:T(8,128)(2,1)}, u32[]{:S(2)}, u32[]{:S(2)}) %collective-permute-start.20) | collective-permute-done | bytes 1048608 | tf_op jit(solution)/shard_map/ppermute | solution.py:404
  191.0 1.4 collective-permute-done.23.refs_2_
  192.4 2.2 collective-permute-start.21
  198.1 20.3 %select.20 = (s32[6,432]{1,0:T(8,128)}, bf16[432,128,128]{2,1,0:T(8,128)(2,1)}) custom-call(s32[8,2,12]{2,1,0:T(2,128)} %bitcast.36, s32[8,2,12]{2,1,0:T(2,128)} %bitcast.37, s32[6]{0:T(128)} %stack.57.refs_2_.meta, bf16[2,2,144,1536]{3,2,1,0:T(8,128)(2,1)} %copy-done, bf16[2,2,144,1536]{3,2,1,0:T(8,128)(2,1)} %copy-done.2, ...), custom_call_target="tpu_custom_call" | custom-call | tf_op jit(solution)/shard_map/select/pallas_call | solution.py:285
  219.4 12.5 %project.2.refs_4_ = f32[4,12,128,256]{3,2,1,0:T(8,128)} custom-call(s32[6,432]{1,0:T(8,128)} %get-tuple-element.20.facts, s32[6]{0:T(128)} %stack.57.refs_2_.meta, bf16[432,128,128]{2,1,0:T(8,128)(2,1)} %get-tuple-element.21.columns, bf16[2,4,2,128,256]{4,3,2,1,0:T(8,128)(2,1)} %pad_maximum_fusion.2.refs_0_, bf16[2,4,2,128,256]{4,3,2,1,0:T(8,128)(2,1)} %copy-done.21, ...), custom_call_target="tpu_custom_call" | custom-call | tf_op jit(solution)/shard_map/project/pallas_call | solution.py:385
  233.0 15.1 %project.3 = f32[4,3072,128]{2,1,0:T(8,128)} custom-call(s32[6,432]{1,0:T(8,128)} %get-tuple-element.20.facts, s32[6]{0:T(128)} %stack.57.refs_2_.meta, bf16[432,128,128]{2,1,0:T(8,128)(2,1)} %get-tuple-element.21.columns, bf16[2,4,2,128,256]{4,3,2,1,0:T(8,128)(2,1)} %collective-permute-done.20.refs_0_, ...), custom_call_target="tpu_custom_call" | custom-call | tf_op jit(solution)/shard_map/project/pallas_call | solution.py:385
  (133 shorter events, 27.0 us)
Async XLA Ops:
  10.8 20.7 %collective-permute-start = (bf16[1,2,144,1536]{3,2,1,0:T(8,128)(2,1)S(1)}, bf16[1,2,144,1536]{3,2,1,0:T(8,128)(2,1)}, u32[]{:S(2)}, u32[]{:S(2)}) collective-permute-start(bf16[1,2,144,1536]{3,2,1,0:T(8,128)(2,1)S(1)} %get-tuple-element.30), channel_id=1, source_target_pairs={{0,8},{4,12},{8,0},{12,4},{16,24},{20,28},{24,16},{28,20},{1,9},{5... | collective-permute-start | bytes 2654216 | tf_op jit(solution)/shard_map/ppermute | solution.py:404
  12.1 55.2 %collective-permute-start.4 = (bf16[1,2,144,1536]{3,2,1,0:T(8,128)(2,1)S(1)}, bf16[1,2,144,1536]{3,2,1,0:T(8,128)(2,1)S(1)}, u32[]{:S(2)}, u32[]{:S(2)}) collective-permute-start(bf16[1,2,144,1536]{3,2,1,0:T(8,128)(2,1)S(1)} %get-tuple-element.29), channel_id=1, source_target_pairs={{0,16},{4,20},{8,24},{12,28},{16,0},{20,4},{24,8},{28,12},{1,17},{... | collective-permute-start | bytes 2654216 | tf_op jit(solution)/shard_map/ppermute | solution.py:404
  18.6 15.5 %collective-permute-start.15 = (bf16[4,128,256]{2,1,0:T(8,128)(2,1)}, bf16[4,128,256]{2,1,0:T(8,128)(2,1)S(1)}, u32[]{:S(2)}, u32[]{:S(2)}) collective-permute-start(bf16[4,128,256]{2,1,0:T(8,128)(2,1)} %get-tuple-element.28), channel_id=1, source_target_pairs={{0,1},{1,0},{2,3},{3,2},{4,5},{5,4},{6,7},{7,6},{8,9},{9,8},{10,11... | collective-permute-start | bytes 786440 | tf_op jit(solution)/shard_map/ppermute | solution.py:404
  32.9 85.4 %collective-permute-start.1 = (bf16[2,2,144,1536]{3,2,1,0:T(8,128)(2,1)S(1)}, bf16[2,2,144,1536]{3,2,1,0:T(8,128)(2,1)S(1)}, u32[]{:S(2)}, u32[]{:S(2)}) collective-permute-start(bf16[2,2,144,1536]{3,2,1,0:T(8,128)(2,1)S(1)} %pad_maximum_fusion.refs_3_.refs_8_), channel_id=1, source_target_pairs={{0,16},{4,20},{8,24},{12,28},{16,0},{20,4},{24,8},{28,12},{1,17},{... | collective-permute-start | bytes 5308424 | tf_op jit(solution)/shard_map/ppermute | solution.py:404
  34.3 31.5 %collective-permute-start.16 = (bf16[4,128,256]{2,1,0:T(8,128)(2,1)S(1)}, bf16[4,128,256]{2,1,0:T(8,128)(2,1)S(1)}, u32[]{:S(2)}, u32[]{:S(2)}) collective-permute-start(bf16[4,128,256]{2,1,0:T(8,128)(2,1)S(1)} %fusion.2), channel_id=1, source_target_pairs={{0,2},{1,3},{2,0},{3,1},{4,6},{5,7},{6,4},{7,5},{8,10},{9,11},{10,... | collective-permute-start | bytes 786440 | tf_op jit(solution)/shard_map/ppermute | solution.py:404
  34.4 38.9 %collective-permute-start.8 = (bf16[12,128,256]{2,1,0:T(8,128)(2,1)S(1)}, bf16[12,128,256]{2,1,0:T(8,128)(2,1)S(1)}, u32[]{:S(2)}, u32[]{:S(2)}) collective-permute-start(bf16[12,128,256]{2,1,0:T(8,128)(2,1)S(1)} %copy-done.28), channel_id=1, source_target_pairs={{0,3},{1,2},{2,1},{3,0},{4,7},{5,6},{6,5},{7,4},{8,11},{9,10},{10,... | collective-permute-start | bytes 2359304 | tf_op jit(solution)/shard_map/ppermute | solution.py:404
  68.2 74.6 %collective-permute-start.5 = (bf16[2,2,144,1536]{3,2,1,0:T(8,128)(2,1)S(1)}, bf16[2,2,144,1536]{3,2,1,0:T(8,128)(2,1)}, u32[]{:S(2)}, u32[]{:S(2)}) collective-permute-start(bf16[2,2,144,1536]{3,2,1,0:T(8,128)(2,1)S(1)} %pad_maximum_fusion.1.refs_7_.refs_8_), channel_id=1, source_target_pairs={{0,8},{4,12},{8,0},{12,4},{16,24},{20,28},{24,16},{28,20},{1,9},{5... | collective-permute-start | bytes 5308424 | tf_op jit(solution)/shard_map/ppermute | solution.py:404
  68.4 47.9 %collective-permute-start.9 = (bf16[12,128,256]{2,1,0:T(8,128)(2,1)S(1)}, bf16[12,128,256]{2,1,0:T(8,128)(2,1)S(1)}, u32[]{:S(2)}, u32[]{:S(2)}) collective-permute-start(bf16[12,128,256]{2,1,0:T(8,128)(2,1)S(1)} %copy-done.27), channel_id=1, source_target_pairs={{0,2},{1,3},{2,0},{3,1},{4,6},{5,7},{6,4},{7,5},{8,10},{9,11},{10,... | collective-permute-start | bytes 2359304 | tf_op jit(solution)/shard_map/ppermute | solution.py:404
  73.3 44.0 %collective-permute-start.10 = (bf16[12,128,256]{2,1,0:T(8,128)(2,1)S(1)}, bf16[12,128,256]{2,1,0:T(8,128)(2,1)S(1)}, u32[]{:S(2)}, u32[]{:S(2)}) collective-permute-start(bf16[12,128,256]{2,1,0:T(8,128)(2,1)S(1)} %copy-done.26), channel_id=1, source_target_pairs={{0,1},{1,0},{2,3},{3,2},{4,5},{5,4},{6,7},{7,6},{8,9},{9,8},{10,11... | collective-permute-start | bytes 2359304 | tf_op jit(solution)/shard_map/ppermute | solution.py:404
  73.3 44.8 %collective-permute-start.14 = (bf16[12,128,256]{2,1,0:T(8,128)(2,1)S(1)}, bf16[12,128,256]{2,1,0:T(8,128)(2,1)S(1)}, u32[]{:S(2)}, u32[]{:S(2)}) collective-permute-start(bf16[12,128,256]{2,1,0:T(8,128)(2,1)S(1)} %copy-done.8), channel_id=1, source_target_pairs={{0,4},{4,0},{8,12},{12,8},{16,20},{20,16},{24,28},{28,24},{1,5},{5... | collective-permute-start | bytes 2359304 | tf_op jit(solution)/shard_map/ppermute | solution.py:404
  117.3 14.4 %collective-permute-start.11 = (bf16[12,128,256]{2,1,0:T(8,128)(2,1)S(1)}, bf16[12,128,256]{2,1,0:T(8,128)(2,1)S(1)}, u32[]{:S(2)}, u32[]{:S(2)}) collective-permute-start(bf16[12,128,256]{2,1,0:T(8,128)(2,1)S(1)} %collective-permute-done.8.refs_0_), channel_id=1, source_target_pairs={{0,4},{4,0},{8,12},{12,8},{16,20},{20,16},{24,28},{28,24},{1,5},{5... | collective-permute-start | bytes 2359304 | tf_op jit(solution)/shard_map/ppermute | solution.py:404
  118.1 13.7 %collective-permute-start.12 = (bf16[12,128,256]{2,1,0:T(8,128)(2,1)S(1)}, bf16[12,128,256]{2,1,0:T(8,128)(2,1)S(1)}, u32[]{:S(2)}, u32[]{:S(2)}) collective-permute-start(bf16[12,128,256]{2,1,0:T(8,128)(2,1)S(1)} %collective-permute-done.9.refs_1_), channel_id=1, source_target_pairs={{0,4},{4,0},{8,12},{12,8},{16,20},{20,16},{24,28},{28,24},{1,5},{5... | collective-permute-start | bytes 2359304 | tf_op jit(solution)/shard_map/ppermute | solution.py:404
  118.2 13.6 %collective-permute-start.13 = (bf16[12,128,256]{2,1,0:T(8,128)(2,1)S(1)}, bf16[12,128,256]{2,1,0:T(8,128)(2,1)S(1)}, u32[]{:S(2)}, u32[]{:S(2)}) collective-permute-start(bf16[12,128,256]{2,1,0:T(8,128)(2,1)S(1)} %collective-permute-done.10.refs_2_), channel_id=1, source_target_pairs={{0,4},{4,0},{8,12},{12,8},{16,20},{20,16},{24,28},{28,24},{1,5},{5... | collective-permute-start | bytes 2359304 | tf_op jit(solution)/shard_map/ppermute | solution.py:404
  129.4 39.5 %collective-permute-start.2 = (bf16[2,2,144,1536]{3,2,1,0:T(8,128)(2,1)S(1)}, bf16[2,2,144,1536]{3,2,1,0:T(8,128)(2,1)}, u32[]{:S(2)}, u32[]{:S(2)}) collective-permute-start(bf16[2,2,144,1536]{3,2,1,0:T(8,128)(2,1)S(1)} %pad_maximum_fusion.refs_3_.refs_8_), channel_id=1, source_target_pairs={{0,4},{4,0},{8,12},{12,8},{16,20},{20,16},{24,28},{28,24},{1,5},{5... | collective-permute-start | bytes 5308424 | tf_op jit(solution)/shard_map/ppermute | solution.py:404
  131.8 38.7 %collective-permute-start.6 = (bf16[2,2,144,1536]{3,2,1,0:T(8,128)(2,1)S(1)}, bf16[2,2,144,1536]{3,2,1,0:T(8,128)(2,1)}, u32[]{:S(2)}, u32[]{:S(2)}) collective-permute-start(bf16[2,2,144,1536]{3,2,1,0:T(8,128)(2,1)S(1)} %pad_maximum_fusion.1.refs_7_.refs_8_), channel_id=1, source_target_pairs={{0,4},{4,0},{8,12},{12,8},{16,20},{20,16},{24,28},{28,24},{1,5},{5... | collective-permute-start | bytes 5308424 | tf_op jit(solution)/shard_map/ppermute | solution.py:404
  145.0 49.5 %collective-permute-start.3 = (bf16[2,2,144,1536]{3,2,1,0:T(8,128)(2,1)S(1)}, bf16[2,2,144,1536]{3,2,1,0:T(8,128)(2,1)}, u32[]{:S(2)}, u32[]{:S(2)}) collective-permute-start(bf16[2,2,144,1536]{3,2,1,0:T(8,128)(2,1)S(1)} %copy-done.3), channel_id=1, source_target_pairs={{0,4},{4,0},{8,12},{12,8},{16,20},{20,16},{24,28},{28,24},{1,5},{5... | collective-permute-start | bytes 5308424 | tf_op jit(solution)/shard_map/ppermute | solution.py:404
  153.8 13.8 %collective-permute-start.22 = (bf16[1,4,2,128,256]{4,3,2,1,0:T(8,128)(2,1)}, bf16[1,4,2,128,256]{4,3,2,1,0:T(8,128)(2,1)S(1)}, u32[]{:S(2)}, u32[]{:S(2)}) collective-permute-start(bf16[1,4,2,128,256]{4,3,2,1,0:T(8,128)(2,1)} %bitcast.32), channel_id=1, source_target_pairs={{0,16},{4,20},{8,24},{12,28},{16,0},{20,4},{24,8},{28,12},{1,17},{... | collective-permute-start | bytes 1572872 | tf_op jit(solution)/shard_map/ppermute | solution.py:404
  157.2 33.0 %collective-permute-start.20 = (bf16[2,4,2,128,256]{4,3,2,1,0:T(8,128)(2,1)}, bf16[2,4,2,128,256]{4,3,2,1,0:T(8,128)(2,1)}, u32[]{:S(2)}, u32[]{:S(2)}) collective-permute-start(bf16[2,4,2,128,256]{4,3,2,1,0:T(8,128)(2,1)} %pad_maximum_fusion.2.refs_0_), channel_id=1, source_target_pairs={{0,16},{4,20},{8,24},{12,28},{16,0},{20,4},{24,8},{28,12},{1,17},{... | collective-permute-start | bytes 3145736 | tf_op jit(solution)/shard_map/ppermute | solution.py:404
  168.7 23.7 %collective-permute-start.23 = (bf16[2,4,2,128,256]{4,3,2,1,0:T(8,128)(2,1)}, bf16[2,4,2,128,256]{4,3,2,1,0:T(8,128)(2,1)}, u32[]{:S(2)}, u32[]{:S(2)}) collective-permute-start(bf16[2,4,2,128,256]{4,3,2,1,0:T(8,128)(2,1)} %pad_maximum_fusion.3.refs_2_), channel_id=1, source_target_pairs={{0,8},{4,12},{8,0},{12,4},{16,24},{20,28},{24,16},{28,20},{1,9},{5... | collective-permute-start | bytes 3145736 | tf_op jit(solution)/shard_map/ppermute | solution.py:404
  168.9 27.8 %collective-permute-start.7 = (bf16[2,2,144,1536]{3,2,1,0:T(8,128)(2,1)}, bf16[2,2,144,1536]{3,2,1,0:T(8,128)(2,1)S(1)}, u32[]{:S(2)}, u32[]{:S(2)}) collective-permute-start(bf16[2,2,144,1536]{3,2,1,0:T(8,128)(2,1)} %collective-permute-done.5.refs_8_.refs_9_), channel_id=1, source_target_pairs={{0,4},{4,0},{8,12},{12,8},{16,20},{20,16},{24,28},{28,24},{1,5},{5... | collective-permute-start | bytes 5308424 | tf_op jit(solution)/shard_map/ppermute | solution.py:404
  170.5 47.9 %collective-permute-start.25 = (bf16[2,4,2,128,256]{4,3,2,1,0:T(8,128)(2,1)}, bf16[2,4,2,128,256]{4,3,2,1,0:T(8,128)(2,1)S(1)}, u32[]{:S(2)}, u32[]{:S(2)}) collective-permute-start(bf16[2,4,2,128,256]{4,3,2,1,0:T(8,128)(2,1)} %pad_maximum_fusion.2.refs_0_), channel_id=1, source_target_pairs={{0,4},{4,0},{8,12},{12,8},{16,20},{20,16},{24,28},{28,24},{1,5},{5... | collective-permute-start | bytes 3145736 | tf_op jit(solution)/shard_map/ppermute | solution.py:404
  190.2 28.3 %collective-permute-start.26 = (bf16[2,4,2,128,256]{4,3,2,1,0:T(8,128)(2,1)}, bf16[2,4,2,128,256]{4,3,2,1,0:T(8,128)(2,1)}, u32[]{:S(2)}, u32[]{:S(2)}) collective-permute-start(bf16[2,4,2,128,256]{4,3,2,1,0:T(8,128)(2,1)} %pad_maximum_fusion.3.refs_2_), channel_id=1, source_target_pairs={{0,4},{4,0},{8,12},{12,8},{16,20},{20,16},{24,28},{28,24},{1,5},{5... | collective-permute-start | bytes 3145736 | tf_op jit(solution)/shard_map/ppermute | solution.py:404
  192.4 39.5 %collective-permute-start.21 = (bf16[2,4,2,128,256]{4,3,2,1,0:T(8,128)(2,1)}, bf16[2,4,2,128,256]{4,3,2,1,0:T(8,128)(2,1)}, u32[]{:S(2)}, u32[]{:S(2)}) collective-permute-start(bf16[2,4,2,128,256]{4,3,2,1,0:T(8,128)(2,1)} %collective-permute-done.20.refs_0_), channel_id=1, source_target_pairs={{0,4},{4,0},{8,12},{12,8},{16,20},{20,16},{24,28},{28,24},{1,5},{5... | collective-permute-start | bytes 3145736 | tf_op jit(solution)/shard_map/ppermute | solution.py:404
  194.5 37.4 %collective-permute-start.24 = (bf16[2,4,2,128,256]{4,3,2,1,0:T(8,128)(2,1)}, bf16[2,4,2,128,256]{4,3,2,1,0:T(8,128)(2,1)S(1)}, u32[]{:S(2)}, u32[]{:S(2)}) collective-permute-start(bf16[2,4,2,128,256]{4,3,2,1,0:T(8,128)(2,1)} %collective-permute-done.23.refs_2_), channel_id=1, source_target_pairs={{0,4},{4,0},{8,12},{12,8},{16,20},{20,16},{24,28},{28,24},{1,5},{5... | collective-permute-start | bytes 3145736 | tf_op jit(solution)/shard_map/ppermute | solution.py:404
  (32 other events, 506.6 us)

commit v2 on v1

--- a/solution.py
+++ b/solution.py
@@ -9,7 +9,6 @@
 
 F32 = jnp.float32
 BF16 = jnp.bfloat16
-EXTRA = 16
 PARAMS = pltpu.CompilerParams(vmem_limit_bytes=58 * 1024 * 1024)
 SMEM = pl.BlockSpec(memory_space=pltpu.SMEM)
 VMEM = pl.BlockSpec(memory_space=pltpu.VMEM)
@@ -109,124 +108,110 @@
 
 
 def potential_kernel(sizes, ids, meta, *refs):
-    nt, tmasks, npiece, xmasks, no, omasks, first, count, nlocal, rank = sizes
-    panels, refs = refs[:nt], refs[nt:]
-    values, refs = refs[:npiece], refs[npiece:]
-    occ, refs = refs[:no], refs[no:]
-    kern, out, table, x, left, m, sems = refs
+    tmasks, xmasks, omasks, fmasks, nlocal, rank, nchunk = sizes
+    panels, refs = refs[: len(tmasks)], refs[len(tmasks) :]
+    values, refs = refs[: len(xmasks)], refs[len(xmasks) :]
+    occ, refs = refs[: len(omasks)], refs[len(omasks) :]
+    kern, refs = refs[0], refs[1:]
+    outs, (table, x, left, m, tsems, xsems) = refs[:nchunk], refs[nchunk:]
     nb, blk, width = panels[0].shape
-    nocc = width // 2
-    npts = x.shape[2]
+    count, npts = x.shape[1], x.shape[2]
     sig = ids.shape[2]
     copies = []
-    for i in range(nt):
-        over, side = tmasks[i]
+    for i, (over, side) in enumerate(tmasks):
         at = (meta[3] ^ over) * nlocal + (meta[4] ^ side) * nb
-        copies.append(pltpu.make_async_copy(panels[i], table.at[pl.ds(at, nb)], sems.at[i]))
-    place = 0
-    for i in range(npiece):
-        size = values[i].shape[0]
-        copies.append(
-            pltpu.make_async_copy(values[i].at[:, :, pl.ds(0, npts)], x.at[pl.ds(place, size)], sems.at[nt + i])
-        )
-        place += size
-    for c in copies:
+        copies.append(pltpu.make_async_copy(panels[i], table.at[pl.ds(at, nb)], tsems.at[i]))
+    loads = []
+    todo = []
+    at = 0
+    groups = len(values) // nchunk
+    for i, piece in enumerate(values):
+        loads.append(pltpu.make_async_copy(piece, x.at[pl.ds(at, piece.shape[0])], xsems.at[i]))
+        for j, mask in enumerate(xmasks[i]):
+            todo += [(i, i // groups, at + j, mask, b) for b in range(count)]
+        at += piece.shape[0]
+    for c in copies + loads:
         c.start()
+    where = {mask: (i, j) for i, masks in enumerate(omasks) for j, mask in enumerate(masks)}
+    dims = (((1,), (1,)), ((), ()))
+
+    def turn_of(mask, b):
+        piece, row = where[mask]
+        og = occ[piece][row, b]
+        half = width // 2
+        return jnp.concatenate([og, jnp.concatenate([-og[:, half:], og[:, :half]], axis=1)], axis=0)
+
     for c in copies:
         c.wait()
-    sources = [m for masks in xmasks for m in masks]
-    where = {m: (i, j) for i, masks in enumerate(omasks) for j, m in enumerate(masks)}
-    dims = (((1,), (1,)), ((), ()))
-    todo = [(p, mask, b) for p, mask in enumerate(sources) for b in range(count)]
-
-    def turn_of(mask, b):
-        piece, row = where[mask]
-        og = occ[piece][row, first + b]
-        return jnp.concatenate([og, jnp.concatenate([-og[:, nocc:], og[:, :nocc]], axis=1)], axis=0)
-
-    for i, (p, mask, b) in enumerate(todo):
+    seen = -1
+    for i, (piece, chunk, row, mask, b) in enumerate(todo):
+        if piece != seen:
+            loads[piece].wait()
+            seen = piece
+        f = fmasks.index(mask)
         dens = jnp.zeros((npts, width), F32)
         for s in range(0, sig, 2):
-            panel = jnp.concatenate([table[ids[p, b, s]], table[ids[p, b, s + 1]]], axis=0)
-            dens += jnp.dot(x[p, b, :, s * blk : (s + 2) * blk], panel, preferred_element_type=F32)
+            two = [table[ids[f, chunk * count + b, s + t]] for t in range(2)]
+            dens += jnp.dot(
+                x[row, b, :, s * blk : (s + 2) * blk], jnp.concatenate(two, axis=0), preferred_element_type=F32
+            )
         left[i] = dens.astype(BF16)
-    for i, (p, mask, b) in enumerate(todo):
-        rho = lax.dot_general(left[i], turn_of(mask, b), dims, preferred_element_type=F32)
-        weight = kern[p, b]
+    for i, (_, chunk, _, mask, b) in enumerate(todo):
+        rho = lax.dot_general(left[i], turn_of(mask, chunk * count + b), dims, preferred_element_type=F32)
+        weight = kern[fmasks.index(mask), chunk * count + b]
         m[i] = (rho * jnp.concatenate([weight, weight], axis=1)).astype(BF16)
-    for i, (p, mask, b) in enumerate(todo):
-        e = jnp.dot(m[i], turn_of(mask, b), preferred_element_type=F32)
-        out[meta[5] ^ (mask // rank), b] = e.astype(BF16)
-
-
-def potential(panels, values, occ, kern, ids, meta, first, nlocal, rank):
+    for i, (_, chunk, _, mask, b) in enumerate(todo):
+        e = jnp.dot(m[i], turn_of(mask, chunk * count + b), preferred_element_type=F32)
+        outs[chunk][meta[5] ^ (mask // rank), b] = e.astype(BF16)
+
+
+def potential(panels, values, occ, kern, ids, fmasks, meta, nlocal, rank):
     tmasks = tuple(m for _, m in panels)
-    xmasks = tuple(tuple(m) for _, m in values)
+    flat = [piece for pieces in values for piece in pieces]
+    xmasks = tuple(tuple(m) for _, m in flat)
     omasks = tuple(tuple(m) for _, m in occ)
-    nsrc, count, sig = ids.shape
-    npts = kern.shape[-1]
-    blk, width = panels[0][0].shape[1:]
-    nt, npiece, no = len(panels), len(values), len(occ)
-    total = nlocal * (nt * panels[0][0].shape[0] // nlocal)
-    sizes = (nt, tmasks, npiece, xmasks, no, omasks, first, count, nlocal, rank)
+    nchunk = len(values)
+    count, npts, span = flat[0][0].shape[1:]
+    nb, blk, width = panels[0][0].shape
+    nsrc = sum(len(m) for m in xmasks) // nchunk
+    sizes = (tmasks, xmasks, omasks, tuple(fmasks), nlocal, rank, nchunk)
+    out = jax.ShapeDtypeStruct((nsrc, count, npts, width), BF16)
     return pl.pallas_call(
         functools.partial(potential_kernel, sizes),
-        out_shape=jax.ShapeDtypeStruct((nsrc, count, npts, width), BF16),
-        in_specs=[SMEM, SMEM] + [ANY] * (nt + npiece) + [VMEM] * (no + 1),
-        out_specs=VMEM,
+        out_shape=(out,) * nchunk,
+        in_specs=[SMEM, SMEM] + [ANY] * (len(panels) + len(flat)) + [VMEM] * (len(occ) + 1),
+        out_specs=(VMEM,) * nchunk,
         scratch_shapes=[
-            pltpu.VMEM((total, blk, width), BF16),
-            pltpu.VMEM((nsrc, count, npts, sig * blk), BF16),
-            pltpu.VMEM((nsrc * count, npts, width), BF16),
-            pltpu.VMEM((nsrc * count, npts, 2 * npts), BF16),
-            pltpu.SemaphoreType.DMA((nt + npiece,)),
+            pltpu.VMEM((len(panels) * nb, blk, width), BF16),
+            pltpu.VMEM((nchunk * nsrc, count, npts, span), BF16),
+            pltpu.VMEM((nchunk * nsrc * count, npts, width), BF16),
+            pltpu.VMEM((nchunk * nsrc * count, npts, 2 * npts), BF16),
+            pltpu.SemaphoreType.DMA((len(panels),)),
+            pltpu.SemaphoreType.DMA((len(flat),)),
         ],
         compiler_params=PARAMS,
         name="potential",
-    )(ids, meta, *[a for a, _ in panels], *[a for a, _ in values], *[a for a, _ in occ], kern)
-
-
-def select_kernel(sizes, *refs):
-    ncall, xmasks, rank, nown, group = sizes
-    all_ids, refs = refs[:ncall], refs[ncall:]
-    meta, refs = refs[0], refs[1:]
-    values, (facts, columns, x, rows, place, xsems, osems) = refs[: len(xmasks)], refs[len(xmasks) :]
-    sig = all_ids[0].shape[2]
-    npts = x.shape[2]
-    blk = x.shape[3] // sig
-    copies = []
-    at = 0
-    entries = []
-    groups = len(values) // ncall
-    for i, piece in enumerate(values):
-        size = piece.shape[0]
-        copies.append(pltpu.make_async_copy(piece.at[:, :, pl.ds(0, npts)], x.at[pl.ds(at, size)], xsems.at[i]))
-        if i % groups == 0:
-            p = 0
-        for j, mask in enumerate(xmasks[i]):
-            entries += [(i // groups, p, mask, b, at + j) for b in range(x.shape[1])]
-            p += 1
-        at += size
-    for c in copies:
-        c.start()
-    nlist = nown * ncall
+    )(ids, meta, *[a for a, _ in panels], *[a for a, _ in flat], *[a for a, _ in occ], kern)
+
+
+def list_kernel(sizes, ids, meta, facts, place):
+    entries, nchunk, rank, nown = sizes
+    sig = ids.shape[2]
+    nlist = nown * nchunk
     for o in range(nlist + 1):
         place[o] = 0
 
-    def slot(chunk, p, b, s):
-        own = all_ids[chunk][p, b, s] - meta[2]
-        return jnp.where((own >= 0) & (own < nown), own * ncall + chunk, nlist)
-
-    def blank(at, own, chunk):
-        facts[0, at] = own
-        facts[1, at] = chunk
-        for f in range(2, 5):
-            facts[f, at] = 0
-        rows[at] = jnp.zeros(rows.shape[1:], BF16)
-
-    for chunk, p, _, b, _ in entries:
+    def slot(f, b, chunk, s):
+        own = ids[f, b, s] - meta[2]
+        return jnp.where((own >= 0) & (own < nown), own * nchunk + chunk, nlist)
+
+    def put(at, *what):
+        for f, one in enumerate(what):
+            facts[f, at] = jnp.int32(one)
+
+    for f, b, _, chunk, _, _ in entries:
         for s in range(sig):
-            own = slot(chunk, p, b, s)
+            own = slot(f, b, chunk, s)
             place[own] = place[own] + 1
     n = jnp.int32(0)
     for o in range(nlist):
@@ -236,34 +221,73 @@
 
         @pl.when(odd == 1)
         def _(at=n + size, o=o):
-            blank(at, o // ncall, o % ncall)
+            put(at, o // nchunk, o % nchunk, 0, 0, 0, -1, 0)
 
         n = n + size + odd
-    blank(n, 0, 0)
-    blank(n + 1, 0, 0)
-    n = n + lax.rem(n, 4)
-    facts[5, 0] = n
+    put(n, 0, 0, 0, 0, 0, -1, 0)
+    put(n + 1, 0, 0, 0, 0, 0, -1, 0)
+    facts[7, 0] = n + lax.rem(n, 4)
+    for f, b, mask, chunk, row, inner in entries:
+        for s in range(sig):
+            own = slot(f, b, chunk, s)
+
+            @pl.when(own < nlist)
+            def _(f=f, b=b, mask=mask, chunk=chunk, row=row, inner=inner, s=s, own=own):
+                to = place[own]
+                place[own] = to + 1
+                put(to, lax.div(own, nchunk), chunk, mask % rank, meta[5] ^ (mask // rank), inner, row, s)
+
+
+def entries_of(xmasks, fmasks, nchunk, count):
+    out = []
+    at = 0
+    groups = len(xmasks) // nchunk
+    for i, masks in enumerate(xmasks):
+        chunk = i // groups
+        for j, mask in enumerate(masks):
+            out += [(fmasks.index(mask), chunk * count + b, mask, chunk, at + j, b) for b in range(count)]
+        at += len(masks)
+    return tuple(out)
+
+
+def pair_list(xmasks, ids, fmasks, meta, rank, nown, nchunk, count, group):
+    nsrc, _, sig = ids.shape
+    most = -(-(nchunk * (nsrc * count * sig + nown) + 4) // group) * group
+    sizes = (entries_of(xmasks, fmasks, nchunk, count), nchunk, rank, nown)
+    return pl.pallas_call(
+        functools.partial(list_kernel, sizes),
+        out_shape=jax.ShapeDtypeStruct((8, most), jnp.int32),
+        in_specs=[SMEM, SMEM],
+        out_specs=SMEM,
+        scratch_shapes=[pltpu.SMEM((nown * nchunk + 1,), jnp.int32)],
+        compiler_params=PARAMS,
+        name="pairs",
+    )(ids, meta)
+
+
+def gather_kernel(group, facts, *refs):
+    values, (columns, x, rows, xsems, osems) = refs[:-5], refs[-5:]
+    blk = rows.shape[1]
+    copies = []
+    at = 0
+    for i, piece in enumerate(values):
+        copies.append(pltpu.make_async_copy(piece, x.at[pl.ds(at, piece.shape[0])], xsems.at[i]))
+        at += piece.shape[0]
+    for c in copies:
+        c.start()
     for c in copies:
         c.wait()
-    for chunk, p, mask, b, row in entries:
-
-        def one(s, carry, chunk=chunk, p=p, mask=mask, b=b, row=row):
-            own = slot(chunk, p, b, s)
-
-            @pl.when(own < nlist)
-            def _():
-                to = place[own]
-                place[own] = to + 1
-                facts[0, to] = lax.div(own, ncall)
-                facts[1, to] = chunk
-                facts[2, to] = mask % rank
-                facts[3, to] = meta[5] ^ (mask // rank)
-                facts[4, to] = b
-                rows[to] = x[row, b, :, pl.ds(pl.multiple_of(s * blk, blk), blk)].T
-
-            return carry
-
-        lax.fori_loop(0, sig, one, 0)
+    n = facts[7, 0]
+
+    def one(i, carry):
+        for t in range(4):
+            row = facts[5, 4 * i + t]
+            start = pl.multiple_of(facts[6, 4 * i + t] * blk, blk)
+            column = x[jnp.maximum(row, 0), facts[4, 4 * i + t], :, pl.ds(start, blk)]
+            rows[4 * i + t] = jnp.where(row >= 0, column, jnp.zeros_like(column)).T
+        return carry
+
+    lax.fori_loop(0, lax.div(n, 4), one, 0)
     outs = [
         pltpu.make_async_copy(rows.at[pl.ds(i * group, group)], columns.at[pl.ds(i * group, group)], osems.at[i])
         for i in range(columns.shape[0] // group)
@@ -276,27 +300,24 @@
                 getattr(c, act)()
 
 
-def select(values, all_ids, meta, rank, nown, npts, group):
-    flat = [piece for pieces in values for piece in pieces]
-    xmasks = tuple(tuple(m) for _, m in flat)
-    nsrc, count, sig = all_ids[0].shape
-    blk = flat[0][0].shape[-1] // sig
-    most = -(-(len(values) * (nsrc * count * sig + nown) + 4) // group) * group
+def gather(values, facts, blk, group):
+    flat = [a for pieces in values for a, _ in pieces]
+    count, npts, span = flat[0].shape[1:]
+    most = facts.shape[1]
     return pl.pallas_call(
-        functools.partial(select_kernel, (len(values), xmasks, rank, nown, group)),
-        out_shape=(jax.ShapeDtypeStruct((6, most), jnp.int32), jax.ShapeDtypeStruct((most, blk, npts), BF16)),
-        in_specs=[SMEM] * (len(values) + 1) + [ANY] * len(flat),
-        out_specs=(SMEM, ANY),
+        functools.partial(gather_kernel, group),
+        out_shape=jax.ShapeDtypeStruct((most, blk, npts), BF16),
+        in_specs=[SMEM] + [ANY] * len(flat),
+        out_specs=ANY,
         scratch_shapes=[
-            pltpu.VMEM((len(values) * nsrc, count, npts, sig * blk), BF16),
+            pltpu.VMEM((sum(a.shape[0] for a in flat), count, npts, span), BF16),
             pltpu.VMEM((most, blk, npts), BF16),
-            pltpu.SMEM((nown * len(values) + 1,), jnp.int32),
             pltpu.SemaphoreType.DMA((len(flat),)),
             pltpu.SemaphoreType.DMA((most // group,)),
         ],
         compiler_params=PARAMS,
-        name="select",
-    )(*all_ids, meta, *[a for a, _ in flat])
+        name="gather",
+    )(facts, *flat)
 
 
 def project_kernel(sizes, facts, meta, columns, *refs):
@@ -304,11 +325,11 @@
     ne = len(emasks)
     potentials, refs = refs[:ne], refs[ne:]
     before = refs[0] if last else None
-    out, x, e, held, esems, xsems = refs[last:]
+    out, x, e, held, staged, esems, xsems, osems = refs[last:]
     nvs = e.shape[2]
     blk = x.shape[1]
     nown = held.shape[1] if last else out.shape[1]
-    n = facts[5, 0]
+    n = facts[7, 0]
     ecopies = []
     place = {}
     for i in range(ne):
@@ -366,10 +387,14 @@
     lax.fori_loop(0, lax.div(n, 4), one, 0)
     if last:
         nocc = out.shape[2]
+        copies = [pltpu.make_async_copy(staged.at[v], out.at[v], osems.at[v]) for v in range(out.shape[0])]
         for v in range(out.shape[0]):
             for o in range(nown):
                 for c in range(2):
-                    out[v, pl.ds(o * 2 * blk + c, blk, stride=2), :] = total[v, o, :, c * nocc : (c + 1) * nocc]
+                    staged[v, pl.ds(o * 2 * blk + c, blk, stride=2), :] = total[v, o, :, c * nocc : (c + 1) * nocc]
+            copies[v].start()
+        for c in copies:
+            c.wait()
 
 
 def project(potentials, facts, columns, meta, before, rank, nown, group):
@@ -386,13 +411,15 @@
         functools.partial(project_kernel, (nchunk, emasks, rank, group, int(last))),
         out_shape=jax.ShapeDtypeStruct(shape, F32),
         in_specs=[SMEM] * 2 + [ANY] * (1 + ne + int(last)),
-        out_specs=VMEM,
+        out_specs=ANY if last else VMEM,
         scratch_shapes=[
             pltpu.VMEM(columns.shape, BF16),
             pltpu.VMEM((nchunk, rank, slots, nv, count, npts, width), BF16),
             pltpu.VMEM((nv, nown, blk, width) if last else (8, 128), F32),
+            pltpu.VMEM(shape if last else (8, 128), F32),
             pltpu.SemaphoreType.DMA((sum(len(m) for _, m in emasks) + 1,)),
             pltpu.SemaphoreType.DMA((columns.shape[0] // group,)),
+            pltpu.SemaphoreType.DMA((nv,)),
         ],
         compiler_params=PARAMS,
         name="project",
@@ -449,25 +476,21 @@
     low_bits = [1 << b for b in range(rank.bit_length() - 1)]
     part_bits = [1 << b for b in range(parts.bit_length() - 1)]
 
-    planes = list(reversed(range(n_ao)))
-    where = jnp.stack([side * nb] + [(ao ^ over) * nv + vector for over in planes]).astype(jnp.int32)
-    rows = pack(trial, where, n_ao, nb, blk)
     panels = []
-    for over, one in zip(planes, rows, strict=True):
-        panels.append((swap(one, "ao", over) if over else one, (over, 0)))
-    own, occupied, colloc, blocks = lax.optimization_barrier((panels[-1][0], occupied, colloc, blocks))
-    panels[-1] = (own, panels[-1][1])
-
-    numbers = [blocks % 128, blocks // 128]
-    numbers = [jnp.pad(a.astype(F32), ((0, 0), (0, npts - sig))) for a in numbers]
-    exact = jnp.concatenate([coords, weights[:, None]], axis=1)
-    extra = jnp.concatenate([jnp.stack(numbers, axis=1)] + thirds(exact), axis=1).astype(BF16)
-    extra = jnp.pad(extra, ((0, 0), (0, EXTRA - extra.shape[1]), (0, span - npts)))
-    payload = jnp.concatenate([colloc, extra], axis=1)
+    far_first = list(reversed(range(n_ao)))
+    for planes in (far_first[:1], far_first[1:]):
+        where = jnp.stack([side * nb] + [(ao ^ over) * nv + vector for over in planes]).astype(jnp.int32)
+        if panels:
+            where, occupied = lax.optimization_barrier((where, occupied))
+        rows = pack(trial, where, len(planes), nb, blk)
+        for over, one in zip(planes, rows, strict=True):
+            panels.append((swap(one, "ao", over) if over else one, (over, 0)))
+
     near = []
     for chunk in range(2):
-        part = payload[None, chunk * count : (chunk + 1) * count]
+        part = colloc[None, chunk * count : (chunk + 1) * count]
         near.append(across([(part, [0])], high_bits[::-1] if chunk else high_bits))
+    far = [within(pieces, low_bits) for pieces in near]
 
     held, send = occupied_part(occupied, colloc, blocks, meta, blk)
     for s in range(n_ao.bit_length() - 1):
@@ -475,26 +498,29 @@
         send = held.astype(BF16)
     occ = across([(send[None], [0])], high_bits)
 
+    numbers = [blocks % 128, blocks // 128]
+    numbers = [jnp.pad(a.astype(F32), ((0, 0), (0, npts - sig))) for a in numbers]
+    exact = jnp.concatenate([coords, weights[:, None]], axis=1)
+    extra = jnp.concatenate([jnp.stack(numbers, axis=1)] + thirds(exact), axis=1).astype(BF16)
+    extra = within(across([(extra[None], [0])], high_bits), low_bits)
+    fmasks = [m for _, masks in extra for m in masks]
+    extra = jnp.concatenate([a for a, _ in extra], axis=0).astype(F32)
+    ids = (extra[:, :, 0, :sig] + 128 * extra[:, :, 1, :sig]).astype(jnp.int32)
+    exact = (extra[:, :, 2:6] + extra[:, :, 6:10] + extra[:, :, 10:14])[: nv]
+    kern = kernel_matrix(exact[:, :, :3], exact[:, :, 3])
+    group = 4 * sig
+    xmasks = [m for pieces in far for _, m in pieces]
+    facts = pair_list(xmasks, ids, fmasks, meta, rank, nown, 2, count, group)
+
     for bit in part_bits:
         panels = panels + [(swap(a, "grid", bit), (over, m ^ bit)) for a, (over, m) in panels]
-    far = [within(pieces, low_bits) for pieces in near]
-
-    def facts_of(pieces):
-        rows = jnp.concatenate([a[:, :, npts:, :npts] for a, _ in pieces], axis=0).astype(F32)
-        ids = (rows[:, :, 0, :sig] + 128 * rows[:, :, 1, :sig]).astype(jnp.int32)
-        return ids, rows[:, :, 2:6] + rows[:, :, 6:10] + rows[:, :, 10:14]
-
+    columns = gather(far, facts, blk, group)
+    parts = potential(panels, near, occ, kern, ids, fmasks, meta, nlocal, rank)
     early, late = [], []
     for chunk in range(2):
-        ids, exact = facts_of(near[chunk])
-        kern = kernel_matrix(exact[:, :, :3], exact[:, :, 3])
-        e = potential(panels, near[chunk], occ, kern, ids, meta, chunk * count, nlocal, rank)
-        pieces = across([(e[None], [0])], high_bits[::-1] if chunk else high_bits)
+        pieces = across([(parts[chunk][None], [0])], high_bits[::-1] if chunk else high_bits)
         early += [(chunk, a, m) for a, m in within(pieces[:1], low_bits)]
         late += [(chunk, a, m) for a, m in within(pieces[1:], low_bits)]
-    group = 4 * sig
-    all_ids = [facts_of(pieces)[0] for pieces in far]
-    facts, columns = select(far, all_ids, meta, rank, nown, npts, group)
     total = project(early, facts, columns, meta, None, rank, nown, group)
     total = project(late, facts, columns, meta, total, rank, nown, group)
     return total.reshape(nv, nown * blk, 2, nocc)

time: 249 us -> 231 us (0.928)
  the two profiles are of different devices: /device:TPU:25 before, /device:TPU:0 now
where the time goes in v2:
time: 231 us; the launch traced here: 227 us
  waiting for transfers between devices  120 us (52%)
  Pallas kernels  67.2 us (29%)
  starting transfers between devices  26.5 us (11%)
  other arithmetic  8.47 us (4%)
  local copies, waits for them, and re-layouts  4.33 us (2%)
    ppermute x31, waiting for transfers between devices, swap(): return lax.ppermute(array, axis, [(i, i ^ bit) for i in range(size)])  120 us
    ppermute x31, starting transfers between devices, swap(): return lax.ppermute(array, axis, [(i, i ^ bit) for i in range(size)])  26.5 us
    pallas_call x2, Pallas kernels, project(): pl.pallas_call(functools.partial(project_kernel, (nchunk, emasks, rank, g...  24.3 us
    pallas_call x2, Pallas kernels, pack(): pl.pallas_call(pack_kernel, out_shape=(jax.ShapeDtypeStruct((nb, blk, 2 *...  11.6 us
    pallas_call x1, Pallas kernels, potential(): pl.pallas_call(functools.partial(potential_kernel, sizes), out_shape=(out...  9.94 us
    pallas_call x1, Pallas kernels, gather(): pl.pallas_call(functools.partial(gather_kernel, group), out_shape=jax.Sha...  9.04 us
    pallas_call x1, Pallas kernels, pair_list(): pl.pallas_call(functools.partial(list_kernel, sizes), out_shape=jax.Shape...  7.75 us
    pallas_call x1, Pallas kernels, occupied_part(): pl.pallas_call(occupied_kernel, out_shape=(jax.ShapeDtypeStruct(shape, F3...  4.66 us
  transfers between devices with their start and end apart: 31, of which 10 were waited for; matrix products, arithmetic and copies ran while one was open for 4% of the time, Pallas kernels for 22%

profile of v2, /device:TPU:0, one launch (start us, length us, event | category | flops | bytes accessed | tf_op | source)
XLA Modules:
  0.0 226.8 jit_solution(10709883232337556973)
XLA Ops:
  1.2 4.7 %occupied.1 = (f32[4,128,256]{2,1,0:T(8,128)}, bf16[4,128,256]{2,1,0:T(8,128)(2,1)}) custom-call(s32[4,12]{1,0:T(4,128)} %ids.1, s32[6]{0:T(128)} %stack.47.meta, bf16[3072,2,128]{2,1,0:T(2,128)(2,1)} %occupied.2, bf16[4,128,1536]{2,1,0:T(8,128)(2,1)} %values.1), custom_call_target="tpu_custom_call" | custom-call | tf_op jit(solution)/shard_map/occupied/pallas_call | solution.py:99
  5.8 3.1 %collective-permute-start.19 = (bf16[4,128,256]{2,1,0:T(8,128)(2,1)}, bf16[4,128,256]{2,1,0:T(8,128)(2,1)S(1)}, u32[]{:S(2)}, u32[]{:S(2)}) collective-permute-start(bf16[4,128,256]{2,1,0:T(8,128)(2,1)} %get-tuple-element.20), channel_id=1, source_target_pairs={{0,1},{1,0},{2,3},{3,2},{4,5},{5,4},{6,7},{7,6},{8,9},{9,8},{10,11... | collective-permute-start | bytes 786440 | tf_op jit(solution)/shard_map/ppermute | solution.py:431
  9.0 1.6 collective-permute-start
  10.6 7.4 %pack.3 = (bf16[12,128,256]{2,1,0:T(8,128)(2,1)}, bf16[12,128,256]{2,1,0:T(8,128)(2,1)}, bf16[12,128,256]{2,1,0:T(8,128)(2,1)}) custom-call(s32[4]{0:T(128)} %pad_add_fusion.1.where, bf16[3072,16,2,128]{3,2,1,0:T(2,128)(2,1)} %trial.3), custom_call_target="tpu_custom_call" | custom-call | tf_op jit(solution)/shard_map/pack/pallas_call | solution.py:59
  18.0 2.7 %collective-permute-start.13 = (bf16[12,128,256]{2,1,0:T(8,128)(2,1)}, bf16[12,128,256]{2,1,0:T(8,128)(2,1)}, u32[]{:S(2)}, u32[]{:S(2)}) collective-permute-start(bf16[12,128,256]{2,1,0:T(8,128)(2,1)} %get-tuple-element.15), channel_id=1, source_target_pairs={{0,2},{1,3},{2,0},{3,1},{4,6},{5,7},{6,4},{7,5},{8,10},{9,11},{10,... | collective-permute-start | bytes 2359304 | tf_op jit(solution)/shard_map/ppermute | solution.py:431
  20.8 1.6 collective-permute-start.8
  24.0 4.1 %pack.2 = bf16[12,128,256]{2,1,0:T(8,128)(2,1)} custom-call(s32[2]{0:T(128)} %pad_add_fusion.where, bf16[3072,16,2,128]{3,2,1,0:T(2,128)(2,1)} %trial.3), custom_call_target="tpu_custom_call" | custom-call | tf_op jit(solution)/shard_map/pack/pallas_call | solution.py:59
  28.8 11.2 %collective-permute-done.1 = bf16[2,4,14,128]{3,1,0,2:T(4,128)(2,1)S(1)} collective-permute-done((bf16[2,4,14,128]{3,1,0,2:T(4,128)(2,1)S(1)}, bf16[2,4,14,128]{3,1,0,2:T(4,128)(2,1)S(1)}, u32[]{:S(2)}, u32[]{:S(2)}) %collective-permute-start.1) | collective-permute-done | bytes 28704 | tf_op jit(solution)/shard_map/ppermute | solution.py:431
  40.4 25.6 %collective-permute-done.20 = bf16[4,128,256]{2,1,0:T(8,128)(2,1)S(1)} collective-permute-done((bf16[4,128,256]{2,1,0:T(8,128)(2,1)S(1)}, bf16[4,128,256]{2,1,0:T(8,128)(2,1)S(1)}, u32[]{:S(2)}, u32[]{:S(2)}) %collective-permute-start.20) | collective-permute-done | bytes 262176 | tf_op jit(solution)/shard_map/ppermute | solution.py:431
  69.6 2.6 %collective-permute-start.12 = (bf16[12,128,256]{2,1,0:T(8,128)(2,1)S(1)}, bf16[12,128,256]{2,1,0:T(8,128)(2,1)S(1)}, u32[]{:S(2)}, u32[]{:S(2)}) collective-permute-start(bf16[12,128,256]{2,1,0:T(8,128)(2,1)S(1)} %copy-done.14), channel_id=1, source_target_pairs={{0,3},{1,2},{2,1},{3,0},{4,7},{5,6},{6,5},{7,4},{8,11},{9,10},{10,... | collective-permute-start | bytes 2359304 | tf_op jit(solution)/shard_map/ppermute | solution.py:431
  74.1 6.1 %collective-permute-done.21 = bf16[1,4,128,256]{3,2,1,0:T(8,128)(2,1)S(1)} collective-permute-done((bf16[1,4,128,256]{3,2,1,0:T(8,128)(2,1)S(1)}, bf16[1,4,128,256]{3,2,1,0:T(8,128)(2,1)S(1)}, u32[]{:S(2)}, u32[]{:S(2)}) %collective-permute-start.21) | collective-permute-done | bytes 262176 | tf_op jit(solution)/shard_map/ppermute | solution.py:431
  80.9 1.5 collective-permute-start.5
  82.5 14.6 %collective-permute-done.14.refs_2_ = bf16[12,128,256]{2,1,0:T(8,128)(2,1)S(1)} collective-permute-done((bf16[12,128,256]{2,1,0:T(8,128)(2,1)}, bf16[12,128,256]{2,1,0:T(8,128)(2,1)S(1)}, u32[]{:S(2)}, u32[]{:S(2)}) %collective-permute-start.14) | collective-permute-done | bytes 786464 | tf_op jit(solution)/shard_map/ppermute | solution.py:431
  97.1 1.5 collective-permute-start.22
  99.4 27.9 %collective-permute-done.22.refs_13_ = bf16[2,4,128,256]{3,2,1,0:T(8,128)(2,1)} collective-permute-done((bf16[2,4,128,256]{3,2,1,0:T(8,128)(2,1)S(1)}, bf16[2,4,128,256]{3,2,1,0:T(8,128)(2,1)}, u32[]{:S(2)}, u32[]{:S(2)}) %collective-permute-start.22) | collective-permute-done | bytes 524320 | tf_op jit(solution)/shard_map/ppermute | solution.py:431
  133.4 9.9 %potential.1 = (bf16[4,2,128,256]{3,2,1,0:T(8,128)(2,1)}, bf16[4,2,128,256]{3,2,1,0:T(8,128)(2,1)}) custom-call(s32[8,4,12]{2,1,0:T(4,128)} %fusion.4.ids, s32[6]{0:T(128)} %stack.47.meta, bf16[12,128,256]{2,1,0:T(8,128)(2,1)} %copy-done.15, bf16[12,128,256]{2,1,0:T(8,128)(2,1)} %collective-permute-done.13.refs_1_, bf16[12,128,256]{2,1,0:T(8,128)(2,1)} %copy-done.12, ...), custom_call_target="tpu_custom_call" | custom-call | tf_op jit(solution)/shard_map/potential/pallas_call | solution.py:179
  143.4 1.6 collective-permute-start.26
  146.8 10.7 %collective-permute-done.26 = bf16[1,4,2,128,256]{4,3,2,1,0:T(8,128)(2,1)S(1)} collective-permute-done((bf16[1,4,2,128,256]{4,3,2,1,0:T(8,128)(2,1)}, bf16[1,4,2,128,256]{4,3,2,1,0:T(8,128)(2,1)S(1)}, u32[]{:S(2)}, u32[]{:S(2)}) %collective-permute-start.26) | collective-permute-done | bytes 524320 | tf_op jit(solution)/shard_map/ppermute | solution.py:431
  160.2 1.6 collective-permute-start.24
  162.4 20.6 %collective-permute-done.27.refs_2_ = bf16[2,4,2,128,256]{4,3,2,1,0:T(8,128)(2,1)} collective-permute-done((bf16[2,4,2,128,256]{4,3,2,1,0:T(8,128)(2,1)S(1)}, bf16[2,4,2,128,256]{4,3,2,1,0:T(8,128)(2,1)}, u32[]{:S(2)}, u32[]{:S(2)}) %collective-permute-start.27) | collective-permute-done | bytes 1048608 | tf_op jit(solution)/shard_map/ppermute | solution.py:431
  184.3 7.7 %pairs.1.facts = s32[8,432]{1,0:T(8,128)} custom-call(s32[8,4,12]{2,1,0:T(4,128)} %fusion.4.ids, s32[6]{0:T(128)} %stack.47.meta), custom_call_target="tpu_custom_call" | custom-call | tf_op jit(solution)/shard_map/pairs/pallas_call | solution.py:257
  193.3 9.0 %gather.1.columns = bf16[432,128,128]{2,1,0:T(8,128)(2,1)} custom-call(s32[8,432]{1,0:T(8,128)} %pairs.1.facts, bf16[2,2,128,1536]{3,2,1,0:T(8,128)(2,1)} %copy-done.1, bf16[2,2,128,1536]{3,2,1,0:T(8,128)(2,1)} %collective-permute-done.5.refs_1_.refs_9_, bf16[2,2,128,1536]{3,2,1,0:T(8,128)(2,1)} %copy-done.8, bf16[2,2,128,1536]{3,2,1,0:T(8,128)(2,1)} %copy-done.10, ...), custom_call_target="tpu_custom_call" | custom-call | tf_op jit(solution)/shard_map/gather/pallas_call | solution.py:307
  202.4 11.0 %project.2.refs_4_ = f32[4,12,128,256]{3,2,1,0:T(8,128)} custom-call(s32[8,432]{1,0:T(8,128)} %pairs.1.facts, s32[6]{0:T(128)} %stack.47.meta, bf16[432,128,128]{2,1,0:T(8,128)(2,1)} %gather.1.columns, bf16[2,4,2,128,256]{4,3,2,1,0:T(8,128)(2,1)} %copy-done.5, bf16[2,4,2,128,256]{4,3,2,1,0:T(8,128)(2,1)} %collective-permute-done.29.refs_1_, ...), custom_call_target="tpu_custom_call" | custom-call | tf_op jit(solution)/shard_map/project/pallas_call | solution.py:410
  213.4 13.3 %project.3 = f32[4,3072,128]{2,1,0:T(8,128)} custom-call(s32[8,432]{1,0:T(8,128)} %pairs.1.facts, s32[6]{0:T(128)} %stack.47.meta, bf16[432,128,128]{2,1,0:T(8,128)(2,1)} %gather.1.columns, bf16[2,4,2,128,256]{4,3,2,1,0:T(8,128)(2,1)} %collective-permute-done.24.refs_0_, bf16[2,4,2,128,256]{4,3,2,1,0:T(8,128)(2,1)} %collective-permute-done.25.refs_1_, ...), custom_call_target="tpu_custom_call" | custom-call | tf_op jit(solution)/shard_map/project/pallas_call | solution.py:410
  (123 shorter events, 24.6 us)
Async XLA Ops:
  5.8 17.1 %collective-permute-start.19 = (bf16[4,128,256]{2,1,0:T(8,128)(2,1)}, bf16[4,128,256]{2,1,0:T(8,128)(2,1)S(1)}, u32[]{:S(2)}, u32[]{:S(2)}) collective-permute-start(bf16[4,128,256]{2,1,0:T(8,128)(2,1)} %get-tuple-element.20), channel_id=1, source_target_pairs={{0,1},{1,0},{2,3},{3,2},{4,5},{5,4},{6,7},{7,6},{8,9},{9,8},{10,11... | collective-permute-start | bytes 786440 | tf_op jit(solution)/shard_map/ppermute | solution.py:431
  9.0 19.1 %collective-permute-start = (bf16[1,4,14,128]{3,1,0,2:T(4,128)(2,1)S(1)}, bf16[1,4,14,128]{3,1,0,2:T(4,128)(2,1)S(1)}, u32[]{:S(2)}, u32[]{:S(2)}) collective-permute-start(bf16[1,4,14,128]{3,1,0,2:T(4,128)(2,1)S(1)} %get-tuple-element.25), channel_id=1, source_target_pairs={{0,8},{4,12},{8,0},{12,4},{16,24},{20,28},{24,16},{28,20},{1,9},{5... | collective-permute-start | bytes 43016 | tf_op jit(solution)/shard_map/ppermute | solution.py:431
  18.0 62.9 %collective-permute-start.13 = (bf16[12,128,256]{2,1,0:T(8,128)(2,1)}, bf16[12,128,256]{2,1,0:T(8,128)(2,1)}, u32[]{:S(2)}, u32[]{:S(2)}) collective-permute-start(bf16[12,128,256]{2,1,0:T(8,128)(2,1)} %get-tuple-element.15), channel_id=1, source_target_pairs={{0,2},{1,3},{2,0},{3,1},{4,6},{5,7},{6,4},{7,5},{8,10},{9,11},{10,... | collective-permute-start | bytes 2359304 | tf_op jit(solution)/shard_map/ppermute | solution.py:431
  20.8 46.6 %collective-permute-start.8 = (bf16[1,2,128,1536]{3,2,1,0:T(8,128)(2,1)S(1)}, bf16[1,2,128,1536]{3,2,1,0:T(8,128)(2,1)}, u32[]{:S(2)}, u32[]{:S(2)}) collective-permute-start(bf16[1,2,128,1536]{3,2,1,0:T(8,128)(2,1)S(1)} %get-tuple-element.23), channel_id=1, source_target_pairs={{0,16},{4,20},{8,24},{12,28},{16,0},{20,4},{24,8},{28,12},{1,17},{... | collective-permute-start | bytes 2359304 | tf_op jit(solution)/shard_map/ppermute | solution.py:431
  22.4 49.7 %collective-permute-start.4 = (bf16[1,2,128,1536]{3,2,1,0:T(8,128)(2,1)S(1)}, bf16[1,2,128,1536]{3,2,1,0:T(8,128)(2,1)}, u32[]{:S(2)}, u32[]{:S(2)}) collective-permute-start(bf16[1,2,128,1536]{3,2,1,0:T(8,128)(2,1)S(1)} %get-tuple-element.24), channel_id=1, source_target_pairs={{0,8},{4,12},{8,0},{12,4},{16,24},{20,28},{24,16},{28,20},{1,9},{5... | collective-permute-start | bytes 2359304 | tf_op jit(solution)/shard_map/ppermute | solution.py:431
  23.0 43.0 %collective-permute-start.20 = (bf16[4,128,256]{2,1,0:T(8,128)(2,1)S(1)}, bf16[4,128,256]{2,1,0:T(8,128)(2,1)S(1)}, u32[]{:S(2)}, u32[]{:S(2)}) collective-permute-start(bf16[4,128,256]{2,1,0:T(8,128)(2,1)S(1)} %fusion), channel_id=1, source_target_pairs={{0,2},{1,3},{2,0},{3,1},{4,6},{5,7},{6,4},{7,5},{8,10},{9,11},{10,... | collective-permute-start | bytes 786440 | tf_op jit(solution)/shard_map/ppermute | solution.py:431
  39.9 57.1 %collective-permute-start.14 = (bf16[12,128,256]{2,1,0:T(8,128)(2,1)}, bf16[12,128,256]{2,1,0:T(8,128)(2,1)S(1)}, u32[]{:S(2)}, u32[]{:S(2)}) collective-permute-start(bf16[12,128,256]{2,1,0:T(8,128)(2,1)} %get-tuple-element.16), channel_id=1, source_target_pairs={{0,1},{1,0},{2,3},{3,2},{4,5},{5,4},{6,7},{7,6},{8,9},{9,8},{10,11... | collective-permute-start | bytes 2359304 | tf_op jit(solution)/shard_map/ppermute | solution.py:431
  67.2 31.4 %collective-permute-start.18 = (bf16[12,128,256]{2,1,0:T(8,128)(2,1)S(1)}, bf16[12,128,256]{2,1,0:T(8,128)(2,1)S(1)}, u32[]{:S(2)}, u32[]{:S(2)}) collective-permute-start(bf16[12,128,256]{2,1,0:T(8,128)(2,1)S(1)} %copy-done.11), channel_id=1, source_target_pairs={{0,4},{4,0},{8,12},{12,8},{16,20},{20,16},{24,28},{28,24},{1,5},{5... | collective-permute-start | bytes 2359304 | tf_op jit(solution)/shard_map/ppermute | solution.py:431
  69.6 29.3 %collective-permute-start.12 = (bf16[12,128,256]{2,1,0:T(8,128)(2,1)S(1)}, bf16[12,128,256]{2,1,0:T(8,128)(2,1)S(1)}, u32[]{:S(2)}, u32[]{:S(2)}) collective-permute-start(bf16[12,128,256]{2,1,0:T(8,128)(2,1)S(1)} %copy-done.14), channel_id=1, source_target_pairs={{0,3},{1,2},{2,1},{3,0},{4,7},{5,6},{6,5},{7,4},{8,11},{9,10},{10,... | collective-permute-start | bytes 2359304 | tf_op jit(solution)/shard_map/ppermute | solution.py:431
  80.2 50.9 %collective-permute-start.9 = (bf16[2,2,128,1536]{3,2,1,0:T(8,128)(2,1)S(1)}, bf16[2,2,128,1536]{3,2,1,0:T(8,128)(2,1)S(1)}, u32[]{:S(2)}, u32[]{:S(2)}) collective-permute-start(bf16[2,2,128,1536]{3,2,1,0:T(8,128)(2,1)S(1)} %pad_maximum_fusion.1.refs_4_.refs_10_), channel_id=1, source_target_pairs={{0,8},{4,12},{8,0},{12,4},{16,24},{20,28},{24,16},{28,20},{1,9},{5... | collective-permute-start | bytes 4718600 | tf_op jit(solution)/shard_map/ppermute | solution.py:431
  80.9 51.3 %collective-permute-start.5 = (bf16[2,2,128,1536]{3,2,1,0:T(8,128)(2,1)S(1)}, bf16[2,2,128,1536]{3,2,1,0:T(8,128)(2,1)}, u32[]{:S(2)}, u32[]{:S(2)}) collective-permute-start(bf16[2,2,128,1536]{3,2,1,0:T(8,128)(2,1)S(1)} %pad_maximum_fusion.refs_0_.refs_8_), channel_id=1, source_target_pairs={{0,16},{4,20},{8,24},{12,28},{16,0},{20,4},{24,8},{28,12},{1,17},{... | collective-permute-start | bytes 4718600 | tf_op jit(solution)/shard_map/ppermute | solution.py:431
  97.1 30.2 %collective-permute-start.22 = (bf16[2,4,128,256]{3,2,1,0:T(8,128)(2,1)S(1)}, bf16[2,4,128,256]{3,2,1,0:T(8,128)(2,1)}, u32[]{:S(2)}, u32[]{:S(2)}) collective-permute-start(bf16[2,4,128,256]{3,2,1,0:T(8,128)(2,1)S(1)} %pad_maximum_fusion.4.refs_12_), channel_id=1, source_target_pairs={{0,16},{4,20},{8,24},{12,28},{16,0},{20,4},{24,8},{28,12},{1,17},{... | collective-permute-start | bytes 1572872 | tf_op jit(solution)/shard_map/ppermute | solution.py:431
  98.6 29.9 %collective-permute-start.16 = (bf16[12,128,256]{2,1,0:T(8,128)(2,1)}, bf16[12,128,256]{2,1,0:T(8,128)(2,1)S(1)}, u32[]{:S(2)}, u32[]{:S(2)}) collective-permute-start(bf16[12,128,256]{2,1,0:T(8,128)(2,1)} %collective-permute-done.13.refs_1_), channel_id=1, source_target_pairs={{0,4},{4,0},{8,12},{12,8},{16,20},{20,16},{24,28},{28,24},{1,5},{5... | collective-permute-start | bytes 2359304 | tf_op jit(solution)/shard_map/ppermute | solution.py:431
  98.8 32.3 %collective-permute-start.17 = (bf16[12,128,256]{2,1,0:T(8,128)(2,1)S(1)}, bf16[12,128,256]{2,1,0:T(8,128)(2,1)S(1)}, u32[]{:S(2)}, u32[]{:S(2)}) collective-permute-start(bf16[12,128,256]{2,1,0:T(8,128)(2,1)S(1)} %collective-permute-done.14.refs_2_), channel_id=1, source_target_pairs={{0,4},{4,0},{8,12},{12,8},{16,20},{20,16},{24,28},{28,24},{1,5},{5... | collective-permute-start | bytes 2359304 | tf_op jit(solution)/shard_map/ppermute | solution.py:431
  128.6 33.2 %collective-permute-start.10 = (bf16[2,2,128,1536]{3,2,1,0:T(8,128)(2,1)S(1)}, bf16[2,2,128,1536]{3,2,1,0:T(8,128)(2,1)}, u32[]{:S(2)}, u32[]{:S(2)}) collective-permute-start(bf16[2,2,128,1536]{3,2,1,0:T(8,128)(2,1)S(1)} %pad_maximum_fusion.1.refs_4_.refs_10_), channel_id=1, source_target_pairs={{0,4},{4,0},{8,12},{12,8},{16,20},{20,16},{24,28},{28,24},{1,5},{5... | collective-permute-start | bytes 4718600 | tf_op jit(solution)/shard_map/ppermute | solution.py:431
  146.3 15.5 %collective-permute-start.6 = (bf16[2,2,128,1536]{3,2,1,0:T(8,128)(2,1)}, bf16[2,2,128,1536]{3,2,1,0:T(8,128)(2,1)S(1)}, u32[]{:S(2)}, u32[]{:S(2)}) collective-permute-start(bf16[2,2,128,1536]{3,2,1,0:T(8,128)(2,1)} %copy-done.1), channel_id=1, source_target_pairs={{0,4},{4,0},{8,12},{12,8},{16,20},{20,16},{24,28},{28,24},{1,5},{5... | collective-permute-start | bytes 4718600 | tf_op jit(solution)/shard_map/ppermute | solution.py:431
  146.3 16.0 %collective-permute-start.11 = (bf16[2,2,128,1536]{3,2,1,0:T(8,128)(2,1)}, bf16[2,2,128,1536]{3,2,1,0:T(8,128)(2,1)S(1)}, u32[]{:S(2)}, u32[]{:S(2)}) collective-permute-start(bf16[2,2,128,1536]{3,2,1,0:T(8,128)(2,1)} %copy-done.2), channel_id=1, source_target_pairs={{0,4},{4,0},{8,12},{12,8},{16,20},{20,16},{24,28},{28,24},{1,5},{5... | collective-permute-start | bytes 4718600 | tf_op jit(solution)/shard_map/ppermute | solution.py:431
  158.6 24.4 %collective-permute-start.27 = (bf16[2,4,2,128,256]{4,3,2,1,0:T(8,128)(2,1)S(1)}, bf16[2,4,2,128,256]{4,3,2,1,0:T(8,128)(2,1)}, u32[]{:S(2)}, u32[]{:S(2)}) collective-permute-start(bf16[2,4,2,128,256]{4,3,2,1,0:T(8,128)(2,1)S(1)} %pad_maximum_fusion.3.refs_2_), channel_id=1, source_target_pairs={{0,8},{4,12},{8,0},{12,4},{16,24},{20,28},{24,16},{28,20},{1,9},{5... | collective-permute-start | bytes 3145736 | tf_op jit(solution)/shard_map/ppermute | solution.py:431
  160.2 24.1 %collective-permute-start.24 = (bf16[2,4,2,128,256]{4,3,2,1,0:T(8,128)(2,1)S(1)}, bf16[2,4,2,128,256]{4,3,2,1,0:T(8,128)(2,1)}, u32[]{:S(2)}, u32[]{:S(2)}) collective-permute-start(bf16[2,4,2,128,256]{4,3,2,1,0:T(8,128)(2,1)S(1)} %pad_maximum_fusion.2.refs_0_), channel_id=1, source_target_pairs={{0,16},{4,20},{8,24},{12,28},{16,0},{20,4},{24,8},{28,12},{1,17},{... | collective-permute-start | bytes 3145736 | tf_op jit(solution)/shard_map/ppermute | solution.py:431
  161.8 30.3 %collective-permute-start.7 = (bf16[2,2,128,1536]{3,2,1,0:T(8,128)(2,1)}, bf16[2,2,128,1536]{3,2,1,0:T(8,128)(2,1)S(1)}, u32[]{:S(2)}, u32[]{:S(2)}) collective-permute-start(bf16[2,2,128,1536]{3,2,1,0:T(8,128)(2,1)} %collective-permute-done.5.refs_1_.refs_9_), channel_id=1, source_target_pairs={{0,4},{4,0},{8,12},{12,8},{16,20},{20,16},{24,28},{28,24},{1,5},{5... | collective-permute-start | bytes 4718600 | tf_op jit(solution)/shard_map/ppermute | solution.py:431
  161.8 40.6 %collective-permute-start.30 = (bf16[2,4,2,128,256]{4,3,2,1,0:T(8,128)(2,1)S(1)}, bf16[2,4,2,128,256]{4,3,2,1,0:T(8,128)(2,1)}, u32[]{:S(2)}, u32[]{:S(2)}) collective-permute-start(bf16[2,4,2,128,256]{4,3,2,1,0:T(8,128)(2,1)S(1)} %pad_maximum_fusion.3.refs_2_), channel_id=1, source_target_pairs={{0,4},{4,0},{8,12},{12,8},{16,20},{20,16},{24,28},{28,24},{1,5},{5... | collective-permute-start | bytes 3145736 | tf_op jit(solution)/shard_map/ppermute | solution.py:431
  162.3 40.1 %collective-permute-start.29 = (bf16[2,4,2,128,256]{4,3,2,1,0:T(8,128)(2,1)S(1)}, bf16[2,4,2,128,256]{4,3,2,1,0:T(8,128)(2,1)}, u32[]{:S(2)}, u32[]{:S(2)}) collective-permute-start(bf16[2,4,2,128,256]{4,3,2,1,0:T(8,128)(2,1)S(1)} %pad_maximum_fusion.2.refs_0_), channel_id=1, source_target_pairs={{0,4},{4,0},{8,12},{12,8},{16,20},{20,16},{24,28},{28,24},{1,5},{5... | collective-permute-start | bytes 3145736 | tf_op jit(solution)/shard_map/ppermute | solution.py:431
  183.0 30.4 %collective-permute-start.28 = (bf16[2,4,2,128,256]{4,3,2,1,0:T(8,128)(2,1)}, bf16[2,4,2,128,256]{4,3,2,1,0:T(8,128)(2,1)}, u32[]{:S(2)}, u32[]{:S(2)}) collective-permute-start(bf16[2,4,2,128,256]{4,3,2,1,0:T(8,128)(2,1)} %collective-permute-done.27.refs_2_), channel_id=1, source_target_pairs={{0,4},{4,0},{8,12},{12,8},{16,20},{20,16},{24,28},{28,24},{1,5},{5... | collective-permute-start | bytes 3145736 | tf_op jit(solution)/shard_map/ppermute | solution.py:431
  184.3 29.1 %collective-permute-start.25 = (bf16[2,4,2,128,256]{4,3,2,1,0:T(8,128)(2,1)}, bf16[2,4,2,128,256]{4,3,2,1,0:T(8,128)(2,1)}, u32[]{:S(2)}, u32[]{:S(2)}) collective-permute-start(bf16[2,4,2,128,256]{4,3,2,1,0:T(8,128)(2,1)} %collective-permute-done.24.refs_0_), channel_id=1, source_target_pairs={{0,4},{4,0},{8,12},{12,8},{16,20},{20,16},{24,28},{28,24},{1,5},{5... | collective-permute-start | bytes 3145736 | tf_op jit(solution)/shard_map/ppermute | solution.py:431
  (30 other events, 567.3 us)

commit v3 on v2

--- a/solution.py
+++ b/solution.py
@@ -179,7 +179,7 @@
     return pl.pallas_call(
         functools.partial(potential_kernel, sizes),
         out_shape=(out,) * nchunk,
-        in_specs=[SMEM, SMEM] + [ANY] * (len(panels) + len(flat)) + [VMEM] * (len(occ) + 1),
+        in_specs=[SMEM, SMEM] + [VMEM] * len(panels) + [ANY] * len(flat) + [VMEM] * (len(occ) + 1),
         out_specs=(VMEM,) * nchunk,
         scratch_shapes=[
             pltpu.VMEM((len(panels) * nb, blk, width), BF16),
@@ -197,45 +197,37 @@
 def list_kernel(sizes, ids, meta, facts, place):
     entries, nchunk, rank, nown = sizes
     sig = ids.shape[2]
-    nlist = nown * nchunk
-    for o in range(nlist + 1):
-        place[o] = 0
-
-    def slot(f, b, chunk, s):
-        own = ids[f, b, s] - meta[2]
-        return jnp.where((own >= 0) & (own < nown), own * nchunk + chunk, nlist)
-
-    def put(at, *what):
-        for f, one in enumerate(what):
-            facts[f, at] = jnp.int32(one)
-
-    for f, b, _, chunk, _, _ in entries:
-        for s in range(sig):
-            own = slot(f, b, chunk, s)
-            place[own] = place[own] + 1
+    nlist = nchunk * rank
+    sizes = []
+    for t in range(nlist):
+        n = jnp.int32(0)
+        for f, b, mask, chunk, _, _ in entries:
+            if chunk * rank + mask % rank == t:
+                for s in range(sig):
+                    own = ids[f, b, s] - meta[2]
+                    n = n + ((own >= 0) & (own < nown)).astype(jnp.int32)
+        sizes.append(n)
     n = jnp.int32(0)
-    for o in range(nlist):
-        size = place[o]
-        place[o] = n
-        odd = lax.rem(size, 2)
-
-        @pl.when(odd == 1)
-        def _(at=n + size, o=o):
-            put(at, o // nchunk, o % nchunk, 0, 0, 0, -1, 0)
-
-        n = n + size + odd
-    put(n, 0, 0, 0, 0, 0, -1, 0)
-    put(n + 1, 0, 0, 0, 0, 0, -1, 0)
-    facts[7, 0] = n + lax.rem(n, 4)
+    for t in range(nlist):
+        facts[5, t] = n
+        place[t] = n
+        end = n + sizes[t]
+        for k in range(3):
+            for f, one in enumerate((0, 0, 0, -1, 0)):
+                facts[f, end + k] = jnp.int32(one)
+        n = lax.div(end + 3, 4) * 4
+    facts[5, nlist] = n
     for f, b, mask, chunk, row, inner in entries:
         for s in range(sig):
-            own = slot(f, b, chunk, s)
-
-            @pl.when(own < nlist)
-            def _(f=f, b=b, mask=mask, chunk=chunk, row=row, inner=inner, s=s, own=own):
-                to = place[own]
-                place[own] = to + 1
-                put(to, lax.div(own, nchunk), chunk, mask % rank, meta[5] ^ (mask // rank), inner, row, s)
+            own = ids[f, b, s] - meta[2]
+
+            @pl.when((own >= 0) & (own < nown))
+            def _(mask=mask, t=chunk * rank + mask % rank, row=row, inner=inner, s=s, own=own):
+                to = place[t]
+                place[t] = to + 1
+                what = (own, meta[5] ^ (mask // rank), jnp.int32(inner), jnp.int32(row), jnp.int32(s))
+                for f, one in enumerate(what):
+                    facts[f, to] = one
 
 
 def entries_of(xmasks, fmasks, nchunk, count):
@@ -252,20 +244,20 @@
 
 def pair_list(xmasks, ids, fmasks, meta, rank, nown, nchunk, count, group):
     nsrc, _, sig = ids.shape
-    most = -(-(nchunk * (nsrc * count * sig + nown) + 4) // group) * group
+    most = -(-(nchunk * (nsrc * count * sig + 3 * rank) + 4) // group) * group
     sizes = (entries_of(xmasks, fmasks, nchunk, count), nchunk, rank, nown)
     return pl.pallas_call(
         functools.partial(list_kernel, sizes),
         out_shape=jax.ShapeDtypeStruct((8, most), jnp.int32),
         in_specs=[SMEM, SMEM],
         out_specs=SMEM,
-        scratch_shapes=[pltpu.SMEM((nown * nchunk + 1,), jnp.int32)],
+        scratch_shapes=[pltpu.SMEM((nchunk * rank,), jnp.int32)],
         compiler_params=PARAMS,
         name="pairs",
     )(ids, meta)
 
 
-def gather_kernel(group, facts, *refs):
+def gather_kernel(group, nlist, facts, *refs):
     values, (columns, x, rows, xsems, osems) = refs[:-5], refs[-5:]
     blk = rows.shape[1]
     copies = []
@@ -277,13 +269,13 @@
         c.start()
     for c in copies:
         c.wait()
-    n = facts[7, 0]
+    n = facts[5, nlist]
 
     def one(i, carry):
         for t in range(4):
-            row = facts[5, 4 * i + t]
-            start = pl.multiple_of(facts[6, 4 * i + t] * blk, blk)
-            column = x[jnp.maximum(row, 0), facts[4, 4 * i + t], :, pl.ds(start, blk)]
+            row = facts[3, 4 * i + t]
+            start = pl.multiple_of(facts[4, 4 * i + t] * blk, blk)
+            column = x[jnp.maximum(row, 0), facts[2, 4 * i + t], :, pl.ds(start, blk)]
             rows[4 * i + t] = jnp.where(row >= 0, column, jnp.zeros_like(column)).T
         return carry
 
@@ -300,12 +292,12 @@
                 getattr(c, act)()
 
 
-def gather(values, facts, blk, group):
+def gather(values, facts, blk, group, nlist):
     flat = [a for pieces in values for a, _ in pieces]
     count, npts, span = flat[0].shape[1:]
     most = facts.shape[1]
     return pl.pallas_call(
-        functools.partial(gather_kernel, group),
+        functools.partial(gather_kernel, group, nlist),
         out_shape=jax.ShapeDtypeStruct((most, blk, npts), BF16),
         in_specs=[SMEM] + [ANY] * len(flat),
         out_specs=ANY,
@@ -324,26 +316,11 @@
     nchunk, emasks, rank, group, last = sizes
     ne = len(emasks)
     potentials, refs = refs[:ne], refs[ne:]
-    before = refs[0] if last else None
-    out, x, e, held, staged, esems, xsems, osems = refs[last:]
-    nvs = e.shape[2]
-    blk = x.shape[1]
-    nown = held.shape[1] if last else out.shape[1]
-    n = facts[7, 0]
-    ecopies = []
-    place = {}
-    for i in range(ne):
-        chunk, masks = emasks[i]
-        for j, mask in enumerate(masks):
-            k = place.setdefault((chunk, mask % rank), [])
-            ecopies.append(
-                pltpu.make_async_copy(
-                    potentials[i].at[j], e.at[chunk, mask % rank, len(k)], esems.at[len(ecopies)]
-                )
-            )
-            k.append(mask // rank)
-    if last:
-        ecopies.append(pltpu.make_async_copy(before, held, esems.at[len(ecopies)]))
+    held = refs[0] if last else None
+    out, x, staged, acc, xsems, osems = refs[last:]
+    total = acc if last else out
+    nown, blk = total.shape[1:3]
+    n = facts[5, nchunk * rank]
     xcopies = [
         pltpu.make_async_copy(columns.at[pl.ds(i * group, group)], x.at[pl.ds(i * group, group)], xsems.at[i])
         for i in range(columns.shape[0] // group)
@@ -354,37 +331,31 @@
         def _(c=c):
             c.start()
 
-    for c in ecopies:
-        c.start()
-    total = held if last else out
-    if not last:
-        total[...] = jnp.zeros_like(total)
+    total[...] = held[...] if last else jnp.zeros_like(total)
     for i, c in enumerate(xcopies):
 
         @pl.when(i * group < n)
         def _(c=c):
             c.wait()
 
-    for c in ecopies:
-        c.wait()
-
-    def add(at):
-        own, chunk = facts[0, at], facts[1, at]
-        here = [[facts[f, at + t] for f in range(2, 5)] for t in range(2)]
-        left = jnp.concatenate([x[at], x[at + 1]], axis=1)
-        for k in range(nvs):
-            off = jnp.int32(place[(0, 0)][k])
-            for other in range(1, nchunk):
-                off = jnp.where(chunk == other, place[(other, 0)][k], off)
-            right = jnp.concatenate([e[chunk, side, k, source, b] for side, source, b in here], axis=0)
-            total[meta[5] ^ off, own] += jnp.dot(left, right, preferred_element_type=F32)
-
-    def one(i, carry):
-        add(4 * i)
-        add(4 * i + 2)
-        return carry
-
-    lax.fori_loop(0, lax.div(n, 4), one, 0)
+    for t in range(nchunk * rank):
+        mine = [
+            (i, j, meta[5] ^ (mask // rank))
+            for i, (chunk, masks) in enumerate(emasks)
+            for j, mask in enumerate(masks)
+            if chunk * rank + mask % rank == t
+        ]
+
+        def one(p, carry, mine=mine):
+            for at in range(4):
+                own, source, b = [facts[f, 4 * p + at] for f in range(3)]
+                for i, j, vec in mine:
+                    total[vec, own] += jnp.dot(
+                        x[4 * p + at], potentials[i][j, source, b], preferred_element_type=F32
+                    )
+            return carry
+
+        lax.fori_loop(lax.div(facts[5, t], 4), lax.div(facts[5, t + 1], 4), one, 0)
     if last:
         nocc = out.shape[2]
         copies = [pltpu.make_async_copy(staged.at[v], out.at[v], osems.at[v]) for v in range(out.shape[0])]
@@ -400,24 +371,21 @@
 def project(potentials, facts, columns, meta, before, rank, nown, group):
     emasks = tuple((chunk, tuple(m)) for chunk, _, m in potentials)
     nchunk = 1 + max(chunk for chunk, _, _ in potentials)
-    nv, count, npts, width = potentials[0][1].shape[1:]
+    nv, _, _, width = potentials[0][1].shape[1:]
     blk = columns.shape[1]
     ne = len(potentials)
-    slots = sum(len(m) for _, m in emasks) // nchunk // rank
     last = before is not None
     shape = (nv, nown * blk * 2, width // 2) if last else (nv, nown, blk, width)
     args = [facts, meta, columns, *[a for _, a, _ in potentials]] + ([before] if last else [])
     return pl.pallas_call(
         functools.partial(project_kernel, (nchunk, emasks, rank, group, int(last))),
         out_shape=jax.ShapeDtypeStruct(shape, F32),
-        in_specs=[SMEM] * 2 + [ANY] * (1 + ne + int(last)),
+        in_specs=[SMEM] * 2 + [ANY] + [VMEM] * (ne + int(last)),
         out_specs=ANY if last else VMEM,
         scratch_shapes=[
             pltpu.VMEM(columns.shape, BF16),
-            pltpu.VMEM((nchunk, rank, slots, nv, count, npts, width), BF16),
+            pltpu.VMEM(shape if last else (8, 128), F32),
             pltpu.VMEM((nv, nown, blk, width) if last else (8, 128), F32),
-            pltpu.VMEM(shape if last else (8, 128), F32),
-            pltpu.SemaphoreType.DMA((sum(len(m) for _, m in emasks) + 1,)),
             pltpu.SemaphoreType.DMA((columns.shape[0] // group,)),
             pltpu.SemaphoreType.DMA((nv,)),
         ],
@@ -436,7 +404,8 @@
         got = [(swap(a, "grid", bit), [m ^ bit for m in masks]) for a, masks in pieces]
         if i + 1 < len(bits):
             pieces = [
-                (jnp.concatenate([a, b], axis=0), masks + more) for (a, masks), (b, more) in zip(pieces, got, strict=True)
+                (jnp.concatenate([a, b], axis=0), masks + more)
+                for (a, masks), (b, more) in zip(pieces, got, strict=True)
             ]
         else:
             pieces = pieces + got
@@ -447,13 +416,6 @@
     for bit in bits:
         pieces = pieces + [(swap(a, "grid", bit), [m ^ bit for m in masks]) for a, masks in pieces]
     return pieces
-
-
-def thirds(x):
-    high = lax.reduce_precision(x, 8, 7)
-    rest = x - high
-    mid = lax.reduce_precision(rest, 8, 7)
-    return [high, mid, rest - mid]
 
 
 def on_device(trial, occupied, colloc, blocks, coords, weights):
@@ -494,19 +456,19 @@
 
     held, send = occupied_part(occupied, colloc, blocks, meta, blk)
     for s in range(n_ao.bit_length() - 1):
-        held = held + swap(send, "ao", 1 << s).astype(F32)
+        got = swap(send, "ao", 1 << s)
+        held = held + got.astype(F32)
         send = held.astype(BF16)
-    occ = across([(send[None], [0])], high_bits)
-
-    numbers = [blocks % 128, blocks // 128]
-    numbers = [jnp.pad(a.astype(F32), ((0, 0), (0, npts - sig))) for a in numbers]
-    exact = jnp.concatenate([coords, weights[:, None]], axis=1)
-    extra = jnp.concatenate([jnp.stack(numbers, axis=1)] + thirds(exact), axis=1).astype(BF16)
+        whole = send[None]
+    occ = across([(whole, [0])], high_bits)
+
+    numbers = jnp.pad(blocks.astype(F32), ((0, 0), (0, npts - sig)))
+    extra = jnp.concatenate([numbers[:, None], coords, weights[:, None]], axis=1)
     extra = within(across([(extra[None], [0])], high_bits), low_bits)
     fmasks = [m for _, masks in extra for m in masks]
-    extra = jnp.concatenate([a for a, _ in extra], axis=0).astype(F32)
-    ids = (extra[:, :, 0, :sig] + 128 * extra[:, :, 1, :sig]).astype(jnp.int32)
-    exact = (extra[:, :, 2:6] + extra[:, :, 6:10] + extra[:, :, 10:14])[: nv]
+    extra = jnp.concatenate([a for a, _ in extra], axis=0)
+    ids = extra[:, :, 0, :sig].astype(jnp.int32)
+    exact = extra[:nv, :, 1:]
     kern = kernel_matrix(exact[:, :, :3], exact[:, :, 3])
     group = 4 * sig
     xmasks = [m for pieces in far for _, m in pieces]
@@ -514,7 +476,7 @@
 
     for bit in part_bits:
         panels = panels + [(swap(a, "grid", bit), (over, m ^ bit)) for a, (over, m) in panels]
-    columns = gather(far, facts, blk, group)
+    columns = gather(far, facts, blk, group, 2 * rank)
     parts = potential(panels, near, occ, kern, ids, fmasks, meta, nlocal, rank)
     early, late = [], []
     for chunk in range(2):

time: 231 us -> 229 us (level)
  the two profiles are of different devices: /device:TPU:0 before, /device:TPU:1 now
where the time goes in v3:
time: 229 us
  waiting for transfers between devices  101 us (44%)
  Pallas kernels  69 us (30%)
  starting transfers between devices  43.9 us (19%)
  other arithmetic  10.3 us (4%)
  local copies, waits for them, and re-layouts  4.39 us (2%)
    ppermute x31, waiting for transfers between devices, swap(): return lax.ppermute(array, axis, [(i, i ^ bit) for i in range(size)])  101 us
    ppermute x31, starting transfers between devices, swap(): return lax.ppermute(array, axis, [(i, i ^ bit) for i in range(size)])  43.9 us
    pallas_call x2, Pallas kernels, project(): pl.pallas_call(functools.partial(project_kernel, (nchunk, emasks, rank, g...  28.9 us
    pallas_call x2, Pallas kernels, pack(): pl.pallas_call(pack_kernel, out_shape=(jax.ShapeDtypeStruct((nb, blk, 2 *...  11.6 us
    pallas_call x1, Pallas kernels, gather(): pl.pallas_call(functools.partial(gather_kernel, group, nlist), out_shape=...  9.56 us
    pallas_call x1, Pallas kernels, potential(): pl.pallas_call(functools.partial(potential_kernel, sizes), out_shape=(out...  9.53 us
    pallas_call x1, Pallas kernels, pair_list(): pl.pallas_call(functools.partial(list_kernel, sizes), out_shape=jax.Shape...  4.89 us
    pallas_call x1, Pallas kernels, occupied_part(): pl.pallas_call(occupied_kernel, out_shape=(jax.ShapeDtypeStruct(shape, F3...  4.6 us
  transfers between devices with their start and end apart: 31, of which 8 were waited for; matrix products, arithmetic and copies ran while one was open for 4% of the time, Pallas kernels for 21%

profile of v3, /device:TPU:1, one launch (start us, length us, event | category | flops | bytes accessed | tf_op | source)
XLA Modules:
  0.0 228.9 jit_solution(12711297414820002788)
XLA Ops:
  1.3 4.6 %occupied.1 = (f32[4,128,256]{2,1,0:T(8,128)}, bf16[4,128,256]{2,1,0:T(8,128)(2,1)}) custom-call(s32[4,12]{1,0:T(4,128)} %ids.1, s32[6]{0:T(128)} %stack.45.meta, bf16[3072,2,128]{2,1,0:T(2,128)(2,1)} %occupied.2, bf16[4,128,1536]{2,1,0:T(8,128)(2,1)} %values.1), custom_call_target="tpu_custom_call" | custom-call | tf_op jit(solution)/shard_map/occupied/pallas_call | solution.py:99
  5.9 2.1 collective-permute-start.19
  8.0 7.4 %pack.3 = (bf16[12,128,256]{2,1,0:T(8,128)(2,1)}, bf16[12,128,256]{2,1,0:T(8,128)(2,1)}, bf16[12,128,256]{2,1,0:T(8,128)(2,1)}) custom-call(s32[4]{0:T(128)} %pad_add_fusion.1.where, bf16[3072,16,2,128]{3,2,1,0:T(2,128)(2,1)} %trial.3), custom_call_target="tpu_custom_call" | custom-call | tf_op jit(solution)/shard_map/pack/pallas_call | solution.py:59
  15.5 2.4 %collective-permute-start.13 = (bf16[12,128,256]{2,1,0:T(8,128)(2,1)}, bf16[12,128,256]{2,1,0:T(8,128)(2,1)}, u32[]{:S(2)}, u32[]{:S(2)}) collective-permute-start(bf16[12,128,256]{2,1,0:T(8,128)(2,1)} %get-tuple-element.15), channel_id=1, source_target_pairs={{0,2},{1,3},{2,0},{3,1},{4,6},{5,7},{6,4},{7,5},{8,10},{9,11},{10,... | collective-permute-start | bytes 2359304 | tf_op jit(solution)/shard_map/ppermute | solution.py:399
  22.4 4.1 %pack.2 = bf16[12,128,256]{2,1,0:T(8,128)(2,1)} custom-call(s32[2]{0:T(128)} %pad_add_fusion.where, bf16[3072,16,2,128]{3,2,1,0:T(2,128)(2,1)} %trial.3), custom_call_target="tpu_custom_call" | custom-call | tf_op jit(solution)/shard_map/pack/pallas_call | solution.py:59
  26.5 10.7 %collective-permute-done = f32[1,4,5,128]{3,1,0,2:T(4,128)S(1)} collective-permute-done((f32[1,4,5,128]{3,1,0,2:T(4,128)S(1)}, f32[1,4,5,128]{3,1,0,2:T(4,128)S(1)}, u32[]{:S(2)}, u32[]{:S(2)}) %collective-permute-start) | collective-permute-done | bytes 10272 | tf_op jit(solution)/shard_map/ppermute | solution.py:399
  37.5 26.8 %collective-permute-done.20 = bf16[4,128,256]{2,1,0:T(8,128)(2,1)} collective-permute-done((bf16[4,128,256]{2,1,0:T(8,128)(2,1)}, bf16[4,128,256]{2,1,0:T(8,128)(2,1)}, u32[]{:S(2)}, u32[]{:S(2)}) %collective-permute-start.20) | collective-permute-done | bytes 262176 | tf_op jit(solution)/shard_map/ppermute | solution.py:399
  67.3 1.4 collective-permute-start.18
  73.6 2.4 %collective-permute-start.12 = (bf16[12,128,256]{2,1,0:T(8,128)(2,1)S(1)}, bf16[12,128,256]{2,1,0:T(8,128)(2,1)S(1)}, u32[]{:S(2)}, u32[]{:S(2)}) collective-permute-start(bf16[12,128,256]{2,1,0:T(8,128)(2,1)S(1)} %copy-done.14), channel_id=1, source_target_pairs={{0,3},{1,2},{2,1},{3,0},{4,7},{5,6},{6,5},{7,4},{8,11},{9,10},{10,... | collective-permute-start | bytes 2359304 | tf_op jit(solution)/shard_map/ppermute | solution.py:399
  76.0 2.8 %collective-permute-done.21 = bf16[1,4,128,256]{3,2,1,0:T(8,128)(2,1)S(1)} collective-permute-done((bf16[1,4,128,256]{3,2,1,0:T(8,128)(2,1)S(1)}, bf16[1,4,128,256]{3,2,1,0:T(8,128)(2,1)S(1)}, u32[]{:S(2)}, u32[]{:S(2)}) %collective-permute-start.21) | collective-permute-done | bytes 262176 | tf_op jit(solution)/shard_map/ppermute | solution.py:399
  81.7 15.5 %collective-permute-start.16 = (bf16[12,128,256]{2,1,0:T(8,128)(2,1)}, bf16[12,128,256]{2,1,0:T(8,128)(2,1)S(1)}, u32[]{:S(2)}, u32[]{:S(2)}) collective-permute-start(bf16[12,128,256]{2,1,0:T(8,128)(2,1)} %collective-permute-done.13.refs_1_), channel_id=1, source_target_pairs={{0,4},{4,0},{8,12},{12,8},{16,20},{20,16},{24,28},{28,24},{1,5},{5... | collective-permute-start | bytes 2359304 | tf_op jit(solution)/shard_map/ppermute | solution.py:399
  97.4 28.7 %collective-permute-done.22.refs_13_ = bf16[2,4,128,256]{3,2,1,0:T(8,128)(2,1)} collective-permute-done((bf16[2,4,128,256]{3,2,1,0:T(8,128)(2,1)S(1)}, bf16[2,4,128,256]{3,2,1,0:T(8,128)(2,1)}, u32[]{:S(2)}, u32[]{:S(2)}) %collective-permute-start.22) | collective-permute-done | bytes 524320 | tf_op jit(solution)/shard_map/ppermute | solution.py:399
  126.0 2.1 collective-permute-start.15
  129.4 1.3 rsqrt_multiply_fusion.refs_14_
  133.9 9.5 %potential.1 = (bf16[4,2,128,256]{3,2,1,0:T(8,128)(2,1)}, bf16[4,2,128,256]{3,2,1,0:T(8,128)(2,1)}) custom-call(s32[8,4,12]{2,1,0:T(4,128)} %fusion.2.ids, s32[6]{0:T(128)} %stack.45.meta, bf16[12,128,256]{2,1,0:T(8,128)(2,1)} %copy-done.15, bf16[12,128,256]{2,1,0:T(8,128)(2,1)} %collective-permute-done.13.refs_1_, bf16[12,128,256]{2,1,0:T(8,128)(2,1)} %copy-done.12, ...), custom_call_target="tpu_custom_call" | custom-call | tf_op jit(solution)/shard_map/potential/pallas_call | solution.py:179
  145.9 10.9 %collective-permute-done.26 = bf16[1,4,2,128,256]{4,3,2,1,0:T(8,128)(2,1)S(1)} collective-permute-done((bf16[1,4,2,128,256]{4,3,2,1,0:T(8,128)(2,1)}, bf16[1,4,2,128,256]{4,3,2,1,0:T(8,128)(2,1)S(1)}, u32[]{:S(2)}, u32[]{:S(2)}) %collective-permute-start.26) | collective-permute-done | bytes 524320 | tf_op jit(solution)/shard_map/ppermute | solution.py:399
  158.4 1.3 collective-permute-start.24
  159.7 1.8 collective-permute-start.7
  162.0 19.6 %collective-permute-done.27.refs_2_ = bf16[2,4,2,128,256]{4,3,2,1,0:T(8,128)(2,1)} collective-permute-done((bf16[2,4,2,128,256]{4,3,2,1,0:T(8,128)(2,1)S(1)}, bf16[2,4,2,128,256]{4,3,2,1,0:T(8,128)(2,1)}, u32[]{:S(2)}, u32[]{:S(2)}) %collective-permute-start.27) | collective-permute-done | bytes 1048608 | tf_op jit(solution)/shard_map/ppermute | solution.py:399
  181.6 2.1 collective-permute-start.28
  184.1 4.9 %pairs.1.facts = s32[8,432]{1,0:T(8,128)} custom-call(s32[8,4,12]{2,1,0:T(4,128)} %fusion.2.ids, s32[6]{0:T(128)} %stack.45.meta), custom_call_target="tpu_custom_call" | custom-call | tf_op jit(solution)/shard_map/pairs/pallas_call | solution.py:249
  190.3 9.6 %gather.1.columns = bf16[432,128,128]{2,1,0:T(8,128)(2,1)} custom-call(s32[8,432]{1,0:T(8,128)} %pairs.1.facts, bf16[2,2,128,1536]{3,2,1,0:T(8,128)(2,1)} %copy-done.1, bf16[2,2,128,1536]{3,2,1,0:T(8,128)(2,1)} %collective-permute-done.5.refs_1_.refs_9_, bf16[2,2,128,1536]{3,2,1,0:T(8,128)(2,1)} %copy-done.8, bf16[2,2,128,1536]{3,2,1,0:T(8,128)(2,1)} %copy-done.10, ...), custom_call_target="tpu_custom_call" | custom-call | tf_op jit(solution)/shard_map/gather/pallas_call | solution.py:299
  199.9 13.4 %project.2.refs_4_ = f32[4,12,128,256]{3,2,1,0:T(8,128)} custom-call(s32[8,432]{1,0:T(8,128)} %pairs.1.facts, s32[6]{0:T(128)} %stack.45.meta, bf16[432,128,128]{2,1,0:T(8,128)(2,1)} %gather.1.columns, bf16[2,4,2,128,256]{4,3,2,1,0:T(8,128)(2,1)} %copy-done.5, bf16[2,4,2,128,256]{4,3,2,1,0:T(8,128)(2,1)} %collective-permute-done.29.refs_1_, ...), custom_call_target="tpu_custom_call" | custom-call | tf_op jit(solution)/shard_map/project/pallas_call | solution.py:380
  213.3 15.5 %project.3 = f32[4,3072,128]{2,1,0:T(8,128)} custom-call(s32[8,432]{1,0:T(8,128)} %pairs.1.facts, s32[6]{0:T(128)} %stack.45.meta, bf16[432,128,128]{2,1,0:T(8,128)(2,1)} %gather.1.columns, bf16[2,4,2,128,256]{4,3,2,1,0:T(8,128)(2,1)} %collective-permute-done.24.refs_0_, bf16[2,4,2,128,256]{4,3,2,1,0:T(8,128)(2,1)} %collective-permute-done.25.refs_1_, ...), custom_call_target="tpu_custom_call" | custom-call | tf_op jit(solution)/shard_map/project/pallas_call | solution.py:380
  (118 shorter events, 27.3 us)
Async XLA Ops:
  5.9 14.6 %collective-permute-start.19 = (bf16[4,128,256]{2,1,0:T(8,128)(2,1)}, bf16[4,128,256]{2,1,0:T(8,128)(2,1)S(1)}, u32[]{:S(2)}, u32[]{:S(2)}) collective-permute-start(bf16[4,128,256]{2,1,0:T(8,128)(2,1)} %get-tuple-element.20), channel_id=1, source_target_pairs={{0,1},{1,0},{2,3},{3,2},{4,5},{5,4},{6,7},{7,6},{8,9},{9,8},{10,11... | collective-permute-start | bytes 786440 | tf_op jit(solution)/shard_map/ppermute | solution.py:399
  15.5 64.5 %collective-permute-start.13 = (bf16[12,128,256]{2,1,0:T(8,128)(2,1)}, bf16[12,128,256]{2,1,0:T(8,128)(2,1)}, u32[]{:S(2)}, u32[]{:S(2)}) collective-permute-start(bf16[12,128,256]{2,1,0:T(8,128)(2,1)} %get-tuple-element.15), channel_id=1, source_target_pairs={{0,2},{1,3},{2,0},{3,1},{4,6},{5,7},{6,4},{7,5},{8,10},{9,11},{10,... | collective-permute-start | bytes 2359304 | tf_op jit(solution)/shard_map/ppermute | solution.py:399
  18.0 50.7 %collective-permute-start.8 = (bf16[1,2,128,1536]{3,2,1,0:T(8,128)(2,1)S(1)}, bf16[1,2,128,1536]{3,2,1,0:T(8,128)(2,1)}, u32[]{:S(2)}, u32[]{:S(2)}) collective-permute-start(bf16[1,2,128,1536]{3,2,1,0:T(8,128)(2,1)S(1)} %get-tuple-element.23), channel_id=1, source_target_pairs={{0,16},{4,20},{8,24},{12,28},{16,0},{20,4},{24,8},{28,12},{1,17},{... | collective-permute-start | bytes 2359304 | tf_op jit(solution)/shard_map/ppermute | solution.py:399
  19.3 51.7 %collective-permute-start.4 = (bf16[1,2,128,1536]{3,2,1,0:T(8,128)(2,1)S(1)}, bf16[1,2,128,1536]{3,2,1,0:T(8,128)(2,1)}, u32[]{:S(2)}, u32[]{:S(2)}) collective-permute-start(bf16[1,2,128,1536]{3,2,1,0:T(8,128)(2,1)S(1)} %get-tuple-element.24), channel_id=1, source_target_pairs={{0,8},{4,12},{8,0},{12,4},{16,24},{20,28},{24,16},{28,20},{1,9},{5... | collective-permute-start | bytes 2359304 | tf_op jit(solution)/shard_map/ppermute | solution.py:399
  21.3 43.0 %collective-permute-start.20 = (bf16[4,128,256]{2,1,0:T(8,128)(2,1)}, bf16[4,128,256]{2,1,0:T(8,128)(2,1)}, u32[]{:S(2)}, u32[]{:S(2)}) collective-permute-start(bf16[4,128,256]{2,1,0:T(8,128)(2,1)} %fusion), channel_id=1, source_target_pairs={{0,2},{1,3},{2,0},{3,1},{4,6},{5,7},{6,4},{7,5},{8,10},{9,11},{10,... | collective-permute-start | bytes 786440 | tf_op jit(solution)/shard_map/ppermute | solution.py:399
  21.4 15.9 %collective-permute-start = (f32[1,4,5,128]{3,1,0,2:T(4,128)S(1)}, f32[1,4,5,128]{3,1,0,2:T(4,128)S(1)}, u32[]{:S(2)}, u32[]{:S(2)}) collective-permute-start(f32[1,4,5,128]{3,1,0,2:T(4,128)S(1)} %maximum_bitcast_fusion), channel_id=1, source_target_pairs={{0,8},{4,12},{8,0},{12,4},{16,24},{20,28},{24,16},{28,20},{1,9},{5... | collective-permute-start | bytes 30728 | tf_op jit(solution)/shard_map/ppermute | solution.py:399
  37.3 44.1 %collective-permute-start.14 = (bf16[12,128,256]{2,1,0:T(8,128)(2,1)}, bf16[12,128,256]{2,1,0:T(8,128)(2,1)S(1)}, u32[]{:S(2)}, u32[]{:S(2)}) collective-permute-start(bf16[12,128,256]{2,1,0:T(8,128)(2,1)} %get-tuple-element.16), channel_id=1, source_target_pairs={{0,1},{1,0},{2,3},{3,2},{4,5},{5,4},{6,7},{7,6},{8,9},{9,8},{10,11... | collective-permute-start | bytes 2359304 | tf_op jit(solution)/shard_map/ppermute | solution.py:399
  67.3 14.4 %collective-permute-start.18 = (bf16[12,128,256]{2,1,0:T(8,128)(2,1)S(1)}, bf16[12,128,256]{2,1,0:T(8,128)(2,1)S(1)}, u32[]{:S(2)}, u32[]{:S(2)}) collective-permute-start(bf16[12,128,256]{2,1,0:T(8,128)(2,1)S(1)} %copy-done.11), channel_id=1, source_target_pairs={{0,4},{4,0},{8,12},{12,8},{16,20},{20,16},{24,28},{28,24},{1,5},{5... | collective-permute-start | bytes 2359304 | tf_op jit(solution)/shard_map/ppermute | solution.py:399
  73.6 23.7 %collective-permute-start.12 = (bf16[12,128,256]{2,1,0:T(8,128)(2,1)S(1)}, bf16[12,128,256]{2,1,0:T(8,128)(2,1)S(1)}, u32[]{:S(2)}, u32[]{:S(2)}) collective-permute-start(bf16[12,128,256]{2,1,0:T(8,128)(2,1)S(1)} %copy-done.14), channel_id=1, source_target_pairs={{0,3},{1,2},{2,1},{3,0},{4,7},{5,6},{6,5},{7,4},{8,11},{9,10},{10,... | collective-permute-start | bytes 2359304 | tf_op jit(solution)/shard_map/ppermute | solution.py:399
  78.8 52.8 %collective-permute-start.9 = (bf16[2,2,128,1536]{3,2,1,0:T(8,128)(2,1)S(1)}, bf16[2,2,128,1536]{3,2,1,0:T(8,128)(2,1)S(1)}, u32[]{:S(2)}, u32[]{:S(2)}) collective-permute-start(bf16[2,2,128,1536]{3,2,1,0:T(8,128)(2,1)S(1)} %pad_maximum_fusion.1.refs_4_.refs_10_), channel_id=1, source_target_pairs={{0,8},{4,12},{8,0},{12,4},{16,24},{20,28},{24,16},{28,20},{1,9},{5... | collective-permute-start | bytes 4718600 | tf_op jit(solution)/shard_map/ppermute | solution.py:399
  80.0 52.7 %collective-permute-start.5 = (bf16[2,2,128,1536]{3,2,1,0:T(8,128)(2,1)S(1)}, bf16[2,2,128,1536]{3,2,1,0:T(8,128)(2,1)}, u32[]{:S(2)}, u32[]{:S(2)}) collective-permute-start(bf16[2,2,128,1536]{3,2,1,0:T(8,128)(2,1)S(1)} %pad_maximum_fusion.refs_0_.refs_8_), channel_id=1, source_target_pairs={{0,16},{4,20},{8,24},{12,28},{16,0},{20,4},{24,8},{28,12},{1,17},{... | collective-permute-start | bytes 4718600 | tf_op jit(solution)/shard_map/ppermute | solution.py:399
  81.3 44.7 %collective-permute-start.22 = (bf16[2,4,128,256]{3,2,1,0:T(8,128)(2,1)S(1)}, bf16[2,4,128,256]{3,2,1,0:T(8,128)(2,1)}, u32[]{:S(2)}, u32[]{:S(2)}) collective-permute-start(bf16[2,4,128,256]{3,2,1,0:T(8,128)(2,1)S(1)} %pad_maximum_fusion.4.refs_12_), channel_id=1, source_target_pairs={{0,16},{4,20},{8,24},{12,28},{16,0},{20,4},{24,8},{28,12},{1,17},{... | collective-permute-start | bytes 1572872 | tf_op jit(solution)/shard_map/ppermute | solution.py:399
  81.7 49.1 %collective-permute-start.16 = (bf16[12,128,256]{2,1,0:T(8,128)(2,1)}, bf16[12,128,256]{2,1,0:T(8,128)(2,1)S(1)}, u32[]{:S(2)}, u32[]{:S(2)}) collective-permute-start(bf16[12,128,256]{2,1,0:T(8,128)(2,1)} %collective-permute-done.13.refs_1_), channel_id=1, source_target_pairs={{0,4},{4,0},{8,12},{12,8},{16,20},{20,16},{24,28},{28,24},{1,5},{5... | collective-permute-start | bytes 2359304 | tf_op jit(solution)/shard_map/ppermute | solution.py:399
  97.3 34.3 %collective-permute-start.17 = (bf16[12,128,256]{2,1,0:T(8,128)(2,1)S(1)}, bf16[12,128,256]{2,1,0:T(8,128)(2,1)S(1)}, u32[]{:S(2)}, u32[]{:S(2)}) collective-permute-start(bf16[12,128,256]{2,1,0:T(8,128)(2,1)S(1)} %collective-permute-done.14.refs_2_), channel_id=1, source_target_pairs={{0,4},{4,0},{8,12},{12,8},{16,20},{20,16},{24,28},{28,24},{1,5},{5... | collective-permute-start | bytes 2359304 | tf_op jit(solution)/shard_map/ppermute | solution.py:399
  130.8 28.9 %collective-permute-start.10 = (bf16[2,2,128,1536]{3,2,1,0:T(8,128)(2,1)S(1)}, bf16[2,2,128,1536]{3,2,1,0:T(8,128)(2,1)}, u32[]{:S(2)}, u32[]{:S(2)}) collective-permute-start(bf16[2,2,128,1536]{3,2,1,0:T(8,128)(2,1)S(1)} %pad_maximum_fusion.1.refs_4_.refs_10_), channel_id=1, source_target_pairs={{0,4},{4,0},{8,12},{12,8},{16,20},{20,16},{24,28},{28,24},{1,5},{5... | collective-permute-start | bytes 4718600 | tf_op jit(solution)/shard_map/ppermute | solution.py:399
  145.0 16.5 %collective-permute-start.6 = (bf16[2,2,128,1536]{3,2,1,0:T(8,128)(2,1)}, bf16[2,2,128,1536]{3,2,1,0:T(8,128)(2,1)S(1)}, u32[]{:S(2)}, u32[]{:S(2)}) collective-permute-start(bf16[2,2,128,1536]{3,2,1,0:T(8,128)(2,1)} %copy-done.1), channel_id=1, source_target_pairs={{0,4},{4,0},{8,12},{12,8},{16,20},{20,16},{24,28},{28,24},{1,5},{5... | collective-permute-start | bytes 4718600 | tf_op jit(solution)/shard_map/ppermute | solution.py:399
  145.9 15.7 %collective-permute-start.11 = (bf16[2,2,128,1536]{3,2,1,0:T(8,128)(2,1)}, bf16[2,2,128,1536]{3,2,1,0:T(8,128)(2,1)S(1)}, u32[]{:S(2)}, u32[]{:S(2)}) collective-permute-start(bf16[2,2,128,1536]{3,2,1,0:T(8,128)(2,1)} %copy-done.2), channel_id=1, source_target_pairs={{0,4},{4,0},{8,12},{12,8},{16,20},{20,16},{24,28},{28,24},{1,5},{5... | collective-permute-start | bytes 4718600 | tf_op jit(solution)/shard_map/ppermute | solution.py:399
  158.0 23.7 %collective-permute-start.27 = (bf16[2,4,2,128,256]{4,3,2,1,0:T(8,128)(2,1)S(1)}, bf16[2,4,2,128,256]{4,3,2,1,0:T(8,128)(2,1)}, u32[]{:S(2)}, u32[]{:S(2)}) collective-permute-start(bf16[2,4,2,128,256]{4,3,2,1,0:T(8,128)(2,1)S(1)} %pad_maximum_fusion.3.refs_2_), channel_id=1, source_target_pairs={{0,8},{4,12},{8,0},{12,4},{16,24},{20,28},{24,16},{28,20},{1,9},{5... | collective-permute-start | bytes 3145736 | tf_op jit(solution)/shard_map/ppermute | solution.py:399
  158.4 25.3 %collective-permute-start.24 = (bf16[2,4,2,128,256]{4,3,2,1,0:T(8,128)(2,1)S(1)}, bf16[2,4,2,128,256]{4,3,2,1,0:T(8,128)(2,1)}, u32[]{:S(2)}, u32[]{:S(2)}) collective-permute-start(bf16[2,4,2,128,256]{4,3,2,1,0:T(8,128)(2,1)S(1)} %pad_maximum_fusion.2.refs_0_), channel_id=1, source_target_pairs={{0,16},{4,20},{8,24},{12,28},{16,0},{20,4},{24,8},{28,12},{1,17},{... | collective-permute-start | bytes 3145736 | tf_op jit(solution)/shard_map/ppermute | solution.py:399
  159.7 29.3 %collective-permute-start.7 = (bf16[2,2,128,1536]{3,2,1,0:T(8,128)(2,1)}, bf16[2,2,128,1536]{3,2,1,0:T(8,128)(2,1)S(1)}, u32[]{:S(2)}, u32[]{:S(2)}) collective-permute-start(bf16[2,2,128,1536]{3,2,1,0:T(8,128)(2,1)} %collective-permute-done.5.refs_1_.refs_9_), channel_id=1, source_target_pairs={{0,4},{4,0},{8,12},{12,8},{16,20},{20,16},{24,28},{28,24},{1,5},{5... | collective-permute-start | bytes 4718600 | tf_op jit(solution)/shard_map/ppermute | solution.py:399
  161.5 38.3 %collective-permute-start.30 = (bf16[2,4,2,128,256]{4,3,2,1,0:T(8,128)(2,1)S(1)}, bf16[2,4,2,128,256]{4,3,2,1,0:T(8,128)(2,1)}, u32[]{:S(2)}, u32[]{:S(2)}) collective-permute-start(bf16[2,4,2,128,256]{4,3,2,1,0:T(8,128)(2,1)S(1)} %pad_maximum_fusion.3.refs_2_), channel_id=1, source_target_pairs={{0,4},{4,0},{8,12},{12,8},{16,20},{20,16},{24,28},{28,24},{1,5},{5... | collective-permute-start | bytes 3145736 | tf_op jit(solution)/shard_map/ppermute | solution.py:399
  161.6 38.3 %collective-permute-start.29 = (bf16[2,4,2,128,256]{4,3,2,1,0:T(8,128)(2,1)S(1)}, bf16[2,4,2,128,256]{4,3,2,1,0:T(8,128)(2,1)}, u32[]{:S(2)}, u32[]{:S(2)}) collective-permute-start(bf16[2,4,2,128,256]{4,3,2,1,0:T(8,128)(2,1)S(1)} %pad_maximum_fusion.2.refs_0_), channel_id=1, source_target_pairs={{0,4},{4,0},{8,12},{12,8},{16,20},{20,16},{24,28},{28,24},{1,5},{5... | collective-permute-start | bytes 3145736 | tf_op jit(solution)/shard_map/ppermute | solution.py:399
  181.6 31.6 %collective-permute-start.28 = (bf16[2,4,2,128,256]{4,3,2,1,0:T(8,128)(2,1)}, bf16[2,4,2,128,256]{4,3,2,1,0:T(8,128)(2,1)}, u32[]{:S(2)}, u32[]{:S(2)}) collective-permute-start(bf16[2,4,2,128,256]{4,3,2,1,0:T(8,128)(2,1)} %collective-permute-done.27.refs_2_), channel_id=1, source_target_pairs={{0,4},{4,0},{8,12},{12,8},{16,20},{20,16},{24,28},{28,24},{1,5},{5... | collective-permute-start | bytes 3145736 | tf_op jit(solution)/shard_map/ppermute | solution.py:399
  183.7 29.5 %collective-permute-start.25 = (bf16[2,4,2,128,256]{4,3,2,1,0:T(8,128)(2,1)}, bf16[2,4,2,128,256]{4,3,2,1,0:T(8,128)(2,1)}, u32[]{:S(2)}, u32[]{:S(2)}) collective-permute-start(bf16[2,4,2,128,256]{4,3,2,1,0:T(8,128)(2,1)} %collective-permute-done.24.refs_0_), channel_id=1, source_target_pairs={{0,4},{4,0},{8,12},{12,8},{16,20},{20,16},{24,28},{28,24},{1,5},{5... | collective-permute-start | bytes 3145736 | tf_op jit(solution)/shard_map/ppermute | solution.py:399
  (30 other events, 585.7 us)
